TPU v7x, 32 devices: a whole 2x2x4 slice. The times are simulated.
32 devices in a mesh: row: 8 (over z, x), col: 4 (over y, core).
Axes of the slice: x: 2, y: 2, z: 4, core: 2. Of those that a mesh axis runs over, the one named last changes fastest.
Arguments:
- inverse_tiles: bfloat16 [16384, 16384], P('row', 'col'), may hold values from -0.046875 to 0.046875
- factor: bfloat16 [16384, 4, 512], P('row', None, 'col'), may hold values from -0.75 to 0.75
- inverse_diag: float32 [4, 512, 512], P(None, 'row', 'col'), may hold values from -6 to 6
- tile_list: int32 [4, 128], replicated, may hold values from 0 to 127, as said below
- tile_count: int32 [4], replicated, may hold values from 86 to 128, as said below
Outputs:
- inverse_panel: bfloat16 [16384, 4, 512], P(('row', 'col'))
- diag_block: float32 [4, 512, 512], P(None, 'row', 'col')
Inputs may be any that keep to these rules, and one draw needn't show every extreme that they name: For each supernode the first tile_count entries of tile_list name distinct tiles in increasing order; the remaining entries name the tiles that are not listed. `tile_count`: some supernode lists all 128 tiles.
All inputs are finite; a program needn't handle non-finite values.
Results may differ from a plain program's by a relative error of at most 0.014.
Values may be sent and summed in bfloat16 or wider, within the bound.
No kernel may reach another device: no remote copies, remote signals or barrier semaphores. Data moves between devices by JAX's collectives and lax.ppermute only.
A program may use at most 128 MiB of HBM per device.

v0:
```python
import jax
import jax.numpy as jnp
from jax import lax
from jax.sharding import PartitionSpec as P

TILE = 128


def spread(x, axis, root):
    mine = lax.axis_index(axis) == root
    return lax.psum(jnp.where(mine, x, jnp.zeros_like(x)), axis)


def per_device(inverse_tiles, factor, inverse_diag, tile_list, tile_count):
    row_devices = lax.axis_size("row")
    col_devices = lax.axis_size("col")
    row_index = lax.axis_index("row")
    col_index = lax.axis_index("col")
    rows_blk = inverse_tiles.shape[0]
    cols_blk = inverse_tiles.shape[1]
    supers = factor.shape[1]
    panel_width = factor.shape[2] * col_devices
    share_rows = rows_blk // col_devices
    tile_total = tile_list.shape[1]
    position = jnp.arange(tile_total, dtype=jnp.int32)
    matches = (tile_list[:, :, None] == position[None, None, :]) & (
        position[None, :, None] < tile_count[:, None, None]
    )
    listed = jnp.any(matches, axis=1).astype(jnp.float32)
    live_all = jnp.repeat(listed, TILE, axis=1)
    row_live = lax.dynamic_slice_in_dim(live_all, row_index * rows_blk, rows_blk, 1).T
    row_factor = lax.all_gather(factor, "col", axis=2, tiled=True)
    row_factor = jnp.where(row_live[:, :, None] > 0, row_factor, jnp.zeros_like(row_factor))
    blocks_per = row_devices // col_devices
    received = [
        spread(row_factor, "row", col_index * blocks_per + offset) for offset in range(blocks_per)
    ]
    col_factor = jnp.concatenate(received, axis=0).reshape(cols_blk, supers * panel_width)
    summed = lax.psum_scatter(
        jnp.dot(inverse_tiles, col_factor, preferred_element_type=jnp.float32),
        "col",
        scatter_dimension=0,
        tiled=True,
    )
    share_live = lax.dynamic_slice_in_dim(row_live, col_index * share_rows, share_rows, 0)
    panel_full = -summed.reshape(share_rows, supers, panel_width) * share_live[:, :, None]
    inverse_panel = panel_full.astype(jnp.bfloat16)
    share_factor = lax.dynamic_slice_in_dim(
        row_factor, col_index * share_rows, share_rows, 0
    ).astype(jnp.float32)
    diag_part = jnp.einsum(
        "rsv,rsw->svw", share_factor, panel_full, precision=lax.Precision.HIGHEST
    )
    diag_half = lax.psum_scatter(
        diag_part.astype(jnp.bfloat16), "row", scatter_dimension=1, tiled=True
    )
    diag_mine = lax.psum_scatter(diag_half, "col", scatter_dimension=2, tiled=True).astype(
        jnp.float32
    )
    diag_block = inverse_diag - diag_mine
    return (inverse_panel, diag_block)


def solution(mesh):
    placed = (P("row", "col"), P("row", None, "col"), P(None, "row", "col"), P(), P())
    return jax.shard_map(
        per_device,
        mesh=mesh,
        in_specs=placed,
        out_specs=(P(("row", "col"), None, None), P(None, "row", "col")),
        check_vma=False,
    )
```

profile of v0, /device:TPU:0, one launch (start us, length us, event | category | flops | bytes accessed | tf_op | source)
XLA Modules:
  0.0 900.1 jit_solution(9261894445449556290)
XLA Ops:
  7.2 4.3 copy.15
  11.6 0.7 iota_compare_fusion.1
  12.3 0.9 fusion.9
  13.2 0.1 broadcast_bitcast_fusion
  13.3 0.2 copy.27
  13.5 59.1 %all-gather.2.cloned.1.call-done = bf16[2048,4,512]{0,2,1:T(8,128)(2,1)} async-done(((bf16[2048,4,128]{0,2,1:T(8,128)(2,1)}), bf16[2048,4,512]{0,2,1:T(8,128)(2,1)}) %all-gather.2.cloned.1.call-update) | async-done | bytes 8388624 | tf_op jit(solution)/shard_map/all_gather | solution.py:32
  72.6 9.7 %broadcast_select_fusion.2 = (bf16[2048,4,512]{0,2,1:T(8,128)(2,1)}, bf16[2048,4,512]{0,2,1:T(8,128)(2,1)}) fusion(pred[]{:T(512)S(6)} %eq.19, bf16[2048,4,512]{0,2,1:T(8,128)(2,1)} %all-gather.2.cloned.1.call-done, pred[2048,4]{0,1:T(4,128)(4,1)S(1)} %fusion.10), kind=kLoop, calls=%fused_computation.4 | loop fusion | flops 8388608 | bytes 25174016 | tf_op jit(solution)/shard_map/jit(_where)/select_n | solution.py:11
  82.3 3.8 broadcast_select_fusion
  86.1 513.0 %all-reduce.3.cloned.1.call-done = (bf16[2048,4,512]{0,2,1:T(8,128)(2,1)}, bf16[2048,4,512]{0,2,1:T(8,128)(2,1)}) async-done(((bf16[2048,4,512]{0,2,1:T(8,128)(2,1)}, bf16[2048,4,512]{0,2,1:T(8,128)(2,1)}), (bf16[2048,4,512]{0,2,1:T(8,128)(2,1)}, bf16[2048,4,512]{0,2,1:T(8,128)(2,1)})) %all-reduce.3.cloned.1.call-update) | async-done | bytes 16777232 | tf_op jit(solution)/shard_map/psum | solution.py:11
  599.1 13.8 %pad_maximum_fusion = bf16[4096,4,512]{0,2,1:T(8,128)(2,1)} fusion(bf16[2048,4,512]{0,2,1:T(8,128)(2,1)} %get-tuple-element.2, bf16[2048,4,512]{0,2,1:T(8,128)(2,1)} %get-tuple-element.3), kind=kLoop, calls=%fused_computation | loop fusion | flops 33554432 | bytes 33554432 | tf_op jit(solution)/shard_map/concatenate | solution.py:38
  612.9 43.1 %convolution_bitcast_fusion = f32[2048,2048]{0,1:T(8,128)} fusion(bf16[4096,2048]{0,1:T(8,128)(2,1)} %bitcast.17, bf16[2048,4096]{1,0:T(8,128)(2,1)} %param.5), kind=kOutput, calls=%fused_computation.1 | convolution fusion | flops 34359738368 | bytes 50331648 | tf_op jit(solution)/shard_map/dot_general | solution.py:40
  656.1 0.2 reduce-scatter.8.cloned.1.call-start
  656.4 0.1 copy.16
  656.5 123.6 %reduce-scatter.6.cloned.1.call-done = f32[512,2048]{0,1:T(8,128)} async-done(((f32[2048,2048]{0,1:T(8,128)}), f32[512,2048]{0,1:T(8,128)}) %reduce-scatter.6.cloned.1.call-update) | async-done | bytes 4194320 | tf_op jit(solution)/shard_map/reduce_scatter | solution.py:39
  780.2 4.7 neg.6
  784.8 5.4 copy.17
  790.3 3.9 fusion.12
  794.2 7.0 fusion.3
  801.2 69.0 %reduce-scatter.8.cloned.1.call-done = bf16[4,64,512]{2,1,0:T(8,128)(2,1)} async-done(((bf16[4,512,512]{2,1,0:T(8,128)(2,1)}), bf16[4,64,512]{2,1,0:T(8,128)(2,1)}) %reduce-scatter.8.cloned.1.call-update) | async-done | bytes 262160 | tf_op jit(solution)/shard_map/reduce_scatter | solution.py:54
  870.2 1.3 copy.19
  871.5 1.0 reshape.43
  872.5 19.2 %reduce-scatter.10.cloned.1.call-done = bf16[128,256]{1,0:T(8,128)(2,1)} async-done(((bf16[512,256]{1,0:T(8,128)(2,1)}), bf16[128,256]{1,0:T(8,128)(2,1)}) %reduce-scatter.10.cloned.1.call-update) | async-done | bytes 65552
  891.8 1.0 reshape.44
  892.9 0.7 convert_subtract_fusion
  (15 shorter events, 0.5 us)
Async XLA Ops:
  7.2 65.5 %all-gather.2.cloned.1.call-start = ((), (), s32[]{:S(2)}) async-start(), calls=%async_computation.3 | async-start | bytes 10485760 | tf_op jit(solution)/shard_map/all_gather | solution.py:32
  11.5 587.6 %all-reduce.3.cloned.1.call-start = ((), (), s32[]{:S(2)}) async-start(), calls=%async_computation.7 | async-start | bytes 33554432 | tf_op jit(solution)/shard_map/psum | solution.py:11
  86.1 694.1 %reduce-scatter.6.cloned.1.call-start = ((), (), s32[]{:S(2)}) async-start(), calls=%async_computation.4 | async-start | bytes 20971520 | tf_op jit(solution)/shard_map/reduce_scatter | solution.py:39
  656.1 214.1 %reduce-scatter.8.cloned.1.call-start = ((), (), s32[]{:S(2)}) async-start(), calls=%async_computation.5 | async-start | bytes 2359296 | tf_op jit(solution)/shard_map/reduce_scatter | solution.py:54
  794.2 98.7 %copy-start = (f32[4,64,128]{2,1,0:T(8,128)S(1)}, f32[4,64,128]{2,1,0:T(8,128)}, u32[]{:S(2)}) copy-start(f32[4,64,128]{2,1,0:T(8,128)} %param.7) | copy-start | bytes 393220
  801.2 90.6 %reduce-scatter.10.cloned.1.call-start = ((), (), s32[]{:S(2)}) async-start(), calls=%async_computation.6 | async-start | bytes 327680
Sparse Core Ops, SparseCore 0:
  11.6 60.9 all-gather.1
  86.2 512.8 all-reduce.2
  656.2 123.9 reduce-scatter.5
  801.3 68.8 reduce-scatter.7
  872.6 19.0 reduce-scatter.9
where the time goes:
time: 901 us; the launch traced here: 900 us
  waiting for transfers between devices  784 us (87%)
  matrix products  50.1 us (6%)
  other arithmetic  38.1 us (4%)
  between operations  13.9 us (2%)
  local copies, waits for them, and re-layouts  13.6 us (2%)
    psum x1, waiting for transfers between devices, spread(): return lax.psum(jnp.where(mine, x, jnp.zeros_like(x)), axis)  513 us
    reduce_scatter x1, waiting for transfers between devices, per_device(): lax.psum_scatter(jnp.dot(inverse_tiles, col_factor, preferred_element_typ...  124 us
    reduce_scatter x1, waiting for transfers between devices, per_device(): lax.psum_scatter(diag_part.astype(jnp.bfloat16), 'row', scatter_dimension...  69 us
    all_gather x1, waiting for transfers between devices, per_device(): row_factor = lax.all_gather(factor, 'col', axis=2, tiled=True)  59.1 us
    dot_general x1, matrix products, per_device(): jnp.dot(inverse_tiles, col_factor, preferred_element_type=jnp.float32)  43.1 us
    unnamed x6, waiting for transfers between devices  19.3 us
  transfers between devices with their start and end apart: 5, of which 5 were waited for; matrix products, arithmetic and copies ran while one was open for 0% of the time, Pallas kernels for 0%

commit v1 on v0

v1 whole, which is shorter than its diff:
```python
import functools

import jax
import jax.numpy as jnp
from jax import lax
from jax.experimental import pallas as pl
from jax.experimental.pallas import tpu as pltpu
from jax.sharding import PartitionSpec as P

TILE = 128
AXES = ("row", "col")
LANES = 128


class Grid:
    def __init__(self, rows, cols):
        self.rows, self.cols = rows, cols
        self.per = rows // cols

    def move(self, value, target):
        pairs = []
        for i in range(self.rows):
            for j in range(self.cols):
                to = target(i, j)
                if to is not None:
                    pairs.append((i * self.cols + j, to[0] * self.cols + to[1]))
        return lax.ppermute(value, AXES, pairs)

    def col_swap(self, value, bits):
        return self.move(value, lambda i, j: (i, j ^ bits))

    def row_swap(self, value, bits):
        return self.move(value, lambda i, j: (i ^ bits, j))

    def group_shift(self, value, step, held=0):
        def target(i, j):
            group = i // self.per
            source, to = group - held, group + step
            if 0 <= source < self.cols and 0 <= to < self.cols:
                return (i + step * self.per, j)
            return None

        return self.move(value, target)


def line_gather(grid, own):
    n = grid.cols
    values = {0: own}
    for sign in (1, -1):
        for far in range(1, n):
            if far <= 2:
                values[sign * far] = grid.group_shift(own, sign * far)
            else:
                values[sign * far] = grid.group_shift(
                    values[sign * (far - 1)], sign, held=sign * (far - 1)
                )
    return [values[delta] for delta in range(-(n - 1), n)]


def pick_kernel(n, where_ref, *refs):
    values, outs, sems = refs[: 2 * n - 1], refs[2 * n - 1 : 3 * n - 1], refs[3 * n - 1]
    for d in range(n):
        for k in range(2 * n - 1):

            @pl.when(where_ref[d] == k)
            def _(d=d, k=k):
                pltpu.make_async_copy(values[k], outs[d], sems.at[d]).start()

    for d in range(n):
        pltpu.make_async_copy(values[0], outs[d], sems.at[d]).wait()


def pick(grid, values, where):
    n = grid.cols
    shape = values[0].shape
    if shape[-1] % LANES:
        stacked = jnp.stack(values)
        return [lax.dynamic_index_in_dim(stacked, where[d], 0, keepdims=False) for d in range(n)]
    size = values[0].size * 2
    return pl.pallas_call(
        functools.partial(pick_kernel, n),
        grid_spec=pltpu.PrefetchScalarGridSpec(
            num_scalar_prefetch=1,
            grid=(1,),
            in_specs=[pl.BlockSpec(memory_space=pl.ANY)] * (2 * n - 1),
            out_specs=[pl.BlockSpec(memory_space=pl.ANY)] * n,
            scratch_shapes=[pltpu.SemaphoreType.DMA((n,))],
        ),
        out_shape=[jax.ShapeDtypeStruct(shape, values[0].dtype)] * n,
        cost_estimate=pl.CostEstimate(flops=0, transcendentals=0, bytes_accessed=2 * n * size),
        name="pick",
    )(where, *values)


def panel_kernel(n, per, rows_all, where_ref, a_ref, *refs):
    pieces, refs = refs[: per * n], refs[per * n :]
    left, refs = refs[:n], refs[n:]
    keep, send, diag_keep, diag_send, right, diag, sems = refs
    col, offset, row = where_ref[0], where_ref[1], where_ref[2]
    width = pieces[0].shape[1]
    depth = pieces[0].shape[0]
    part = diag.shape[0] // rows_all
    step = pl.program_id(0)

    @pl.when(step == 0)
    def _():
        copies = []
        for t in range(per):
            for d in range(n):
                place = right.at[
                    pl.ds(pl.multiple_of((offset ^ t) * depth, depth), depth),
                    pl.ds(pl.multiple_of((col ^ d) * width, width), width),
                ]
                copies.append(pltpu.make_async_copy(pieces[t * n + d], place, sems.at[t * n + d]))
        for copy in copies:
            copy.start()
        diag[...] = jnp.zeros_like(diag)
        for copy in copies:
            copy.wait()

    product = jnp.dot(a_ref[...], right[...], preferred_element_type=jnp.float32)
    rounded = product.astype(jnp.bfloat16)

    @pl.when(step % 2 == 0)
    def _():
        keep[0] = product

    @pl.when(step % 2 == 1)
    def _():
        send[0] = rounded

    for d in range(n):
        at = pl.ds(pl.multiple_of((col ^ d) * width, width), width)
        diag[at, :] += lax.dot_general(
            left[d][0], rounded, (((0,), (0,)), ((), ())), preferred_element_type=jnp.float32
        )

    @pl.when(step == n - 1)
    def _():
        for d in range(n):
            at = pl.ds(pl.multiple_of((col ^ d) * width, width), width)
            for block in range(rows_all):
                value = diag[pl.ds(block * part, part), at]
                if d % 2 == 0:
                    diag_keep[d // 2, row ^ block] = value
                else:
                    diag_send[d // 2, row ^ block] = value.astype(jnp.bfloat16)


def panel(grid, where, inverse_tiles, pieces, left, supers):
    n, per, rows_all = grid.cols, grid.per, grid.rows
    col, offset, row = where[0], where[1], where[2]
    depth, width = pieces[0][0].shape[-2:]
    rows_blk, cols_blk = inverse_tiles.shape
    share = rows_blk // n
    panel_width = n * width
    part = panel_width // rows_all
    if width % LANES or len(supers) > 1:
        order_col = col ^ jnp.arange(n)
        order_off = offset ^ jnp.arange(per)
        order_row = row ^ jnp.arange(rows_all)
        right = jnp.stack([jnp.stack(line) for line in pieces])
        right = jnp.take(jnp.take(right, order_off, axis=0), order_col, axis=1)
        right = right.transpose(0, 3, 2, 1, 4).reshape(cols_blk, len(supers) * panel_width)
        product = jnp.dot(inverse_tiles, right, preferred_element_type=jnp.float32)
        product = product.reshape(rows_blk, len(supers), panel_width)
        own = jnp.take(jnp.stack([value[jnp.array(supers)] for value in left]), order_col, axis=0)
        diag = jnp.einsum(
            "dsrv,rsw->sdvw",
            own,
            product.astype(jnp.bfloat16),
            preferred_element_type=jnp.float32,
        )
        diag = diag.reshape(len(supers), rows_all, part, n, width).transpose(3, 1, 0, 2, 4)
        diag = jnp.take(jnp.take(diag, order_col, axis=0), order_row, axis=1)
        product = jnp.take(
            product.reshape(n, share, len(supers), panel_width), order_col, axis=0
        ).transpose(0, 2, 1, 3)
        return (
            product[0::2],
            product[1::2].astype(jnp.bfloat16),
            diag[0::2],
            diag[1::2].astype(jnp.bfloat16),
        )
    half = n // 2
    at = supers[0]
    return pl.pallas_call(
        functools.partial(panel_kernel, n, per, rows_all),
        grid_spec=pltpu.PrefetchScalarGridSpec(
            num_scalar_prefetch=1,
            grid=(n,),
            in_specs=[pl.BlockSpec((share, cols_blk), lambda d, w: (w[0] ^ d, 0))]
            + [pl.BlockSpec(memory_space=pl.ANY)] * (per * n)
            + [pl.BlockSpec((1, share, width), lambda d, w: (at, w[0] ^ d, 0))] * n,
            out_specs=[
                pl.BlockSpec((1, share, panel_width), lambda d, w: (d // 2, 0, 0)),
                pl.BlockSpec((1, share, panel_width), lambda d, w: (d // 2, 0, 0)),
                pl.BlockSpec((half, rows_all, part, width), lambda d, w: (0, 0, 0, 0)),
                pl.BlockSpec((half, rows_all, part, width), lambda d, w: (0, 0, 0, 0)),
            ],
            scratch_shapes=[
                pltpu.VMEM((cols_blk, panel_width), jnp.bfloat16),
                pltpu.VMEM((panel_width, panel_width), jnp.float32),
                pltpu.SemaphoreType.DMA((per * n,)),
            ],
        ),
        out_shape=[
            jax.ShapeDtypeStruct((half, share, panel_width), jnp.float32),
            jax.ShapeDtypeStruct((half, share, panel_width), jnp.bfloat16),
            jax.ShapeDtypeStruct((half, rows_all, part, width), jnp.float32),
            jax.ShapeDtypeStruct((half, rows_all, part, width), jnp.bfloat16),
        ],
        cost_estimate=pl.CostEstimate(
            flops=2 * rows_blk * panel_width * (cols_blk + panel_width),
            transcendentals=0,
            bytes_accessed=2 * rows_blk * cols_blk + 2 * panel_width * (cols_blk + rows_blk) + 3 * rows_blk * panel_width,
        ),
        name="panel",
    )(where, inverse_tiles, *[value for line in pieces for value in line], *left)


def halve_cols(grid, keep, send):
    bit = 1
    while True:
        keep = keep + grid.col_swap(send, bit).astype(jnp.float32)
        bit *= 2
        if bit >= grid.cols:
            return keep[0]
        send, keep = keep[1::2].astype(jnp.bfloat16), keep[0::2]


def halve_rows(grid, value):
    bit = 1
    while bit < grid.rows:
        send, value = value[1::2], value[0::2]
        value = value + grid.row_swap(send, bit)
        bit *= 2
    return value[0]


def per_device(inverse_tiles, factor, inverse_diag, tile_list, tile_count):
    grid = Grid(lax.axis_size("row"), lax.axis_size("col"))
    row = lax.axis_index("row")
    col = lax.axis_index("col")
    group, offset = row // grid.per, row % grid.per
    rows_blk, supers, width = factor.shape
    share = rows_blk // grid.cols
    tiles_blk = rows_blk // TILE

    position = jnp.arange(tile_list.shape[1], dtype=jnp.int32)
    mine = row * tiles_blk + jnp.arange(tiles_blk, dtype=jnp.int32)
    matches = (tile_list[:, None, :] == mine[None, :, None]) & (
        position[None, None, :] < tile_count[:, None, None]
    )
    listed = jnp.any(matches, axis=2)
    live = jnp.repeat(listed, TILE, axis=1)
    masked = jnp.where(
        live[:, :, None], factor.transpose(1, 0, 2), jnp.zeros((), factor.dtype)
    )

    together = 1 if width % LANES == 0 else supers
    chunks = [tuple(range(at, at + together)) for at in range(0, supers, together)]
    where_pick = group - (col ^ jnp.arange(grid.cols, dtype=jnp.int32)) + grid.cols - 1
    where_panel = jnp.stack([col, offset, row]).astype(jnp.int32)

    left = {0: masked}
    bit = grid.cols // 2
    while bit:
        for d in list(left):
            left[d | bit] = grid.col_swap(left[d], bit)
        bit //= 2
    left = [left[d] for d in range(grid.cols)]

    panels, diags = [], []
    for chunk in chunks:
        own = masked[chunk[0]] if len(chunk) == 1 else masked[chunk[0] : chunk[-1] + 1]
        picked = pick(grid, line_gather(grid, own), where_pick)
        line = [picked[0]] + [grid.col_swap(picked[d], d) for d in range(1, grid.cols)]
        pieces = [line] + [
            [grid.row_swap(value, t) for value in line] for t in range(1, grid.per)
        ]
        keep, send, diag_keep, diag_send = panel(
            grid, where_panel, inverse_tiles, pieces, left, chunk
        )
        total = halve_cols(grid, keep, send)
        diag = halve_rows(grid, halve_cols(grid, diag_keep, diag_send))
        panels.append(total.reshape(len(chunk), share, -1))
        diags.append(diag.reshape(len(chunk), -1, width))

    summed = jnp.concatenate(panels, axis=0)
    share_live = lax.dynamic_slice_in_dim(live, col * share, share, 1).astype(jnp.float32)
    inverse_panel = (-summed * share_live[:, :, None]).astype(jnp.bfloat16).transpose(1, 0, 2)
    diag_block = inverse_diag + jnp.concatenate(diags, axis=0)
    return (inverse_panel, diag_block)


def solution(mesh):
    placed = (P("row", "col"), P("row", None, "col"), P(None, "row", "col"), P(), P())
    return jax.shard_map(
        per_device,
        mesh=mesh,
        in_specs=placed,
        out_specs=(P(("row", "col"), None, None), P(None, "row", "col")),
        check_vma=False,
    )
```

time: 901 us -> 749 us (0.83)
  waiting for transfers between devices: 784 us -> 229 us
  Pallas kernels: 0 us -> 338 us
  starting transfers between devices: 0.39 us -> 161 us
  matrix products: 50.1 us -> 0 us
  other arithmetic: 38.1 us -> 13.4 us
  between operations: 13.9 us -> 1.66 us
    psum x1 -> x0, waiting for transfers between devices: 513 us -> none  [spread(): return lax.psum(jnp.where(mine, x, jnp.zeros_like(x)), axis)]
    pallas_call x0 -> x8, Pallas kernels: none -> 338 us  [the longest x4 261 us: pick(): pl.pallas_call(functools.partial(pick_kernel, n), grid_spec=pltpu.Prefetc...]
    ppermute x0 -> x83, waiting for transfers between devices: none -> 229 us  [move(): return lax.ppermute(value, AXES, pairs)]
    reduce_scatter x2 -> x0, waiting for transfers between devices: 193 us -> none  [the longest x1 124 us: per_device(): lax.psum_scatter(jnp.dot(inverse_tiles, col_factor, preferred_element_typ...]
    ppermute x0 -> x83, starting transfers between devices: none -> 161 us  [move(): return lax.ppermute(value, AXES, pairs)]
    all_gather x1 -> x0, waiting for transfers between devices: 59.1 us -> none  [per_device(): row_factor = lax.all_gather(factor, 'col', axis=2, tiled=True)]
    dot_general x2 -> x0, matrix products: 50.1 us -> none  [the longest x1 43.1 us: per_device(): jnp.dot(inverse_tiles, col_factor, preferred_element_type=jnp.float32)]
    unnamed x6 -> x0, waiting for transfers between devices: 19.3 us -> none
  transfers between devices with their start and end apart: 5 -> 83, of which waited for: 5 -> 40; matrix products, arithmetic and copies ran while one was open for 0% -> 1% of each run, Pallas kernels for 0% -> 45%
where the time goes in v1:
time: 749 us
  Pallas kernels  338 us (45%)
  waiting for transfers between devices  229 us (31%)
  starting transfers between devices  161 us (21%)
  other arithmetic  13.4 us (2%)
    pallas_call x4, Pallas kernels, pick(): pl.pallas_call(functools.partial(pick_kernel, n), grid_spec=pltpu.Prefetc...  261 us
    ppermute x83, waiting for transfers between devices, move(): return lax.ppermute(value, AXES, pairs)  229 us
    ppermute x83, starting transfers between devices, move(): return lax.ppermute(value, AXES, pairs)  161 us
    pallas_call x4, Pallas kernels, panel(): pl.pallas_call(functools.partial(panel_kernel, n, per, rows_all), grid_sp...  76.6 us
  transfers between devices with their start and end apart: 83, of which 40 were waited for; matrix products, arithmetic and copies ran while one was open for 1% of the time, Pallas kernels for 45%

profile of v1, /device:TPU:0, one launch (start us, length us, event | category | flops | bytes accessed | tf_op | source)
XLA Modules:
  0.0 748.5 jit_solution(15519540460515338832)
XLA Ops:
  22.3 14.3 %collective-permute-done.48.refs_1_ = bf16[2048,128]{1,0:T(8,128)(2,1)S(1)} collective-permute-done((bf16[2048,128]{1,0:T(8,128)(2,1)S(1)}, bf16[2048,128]{1,0:T(8,128)(2,1)S(1)}, u32[]{:S(2)}, u32[]{:S(2)}) %collective-permute-start.48) | collective-permute-done | bytes 524320 | tf_op jit(solution)/shard_map/ppermute | solution.py:27
  37.9 23.6 %collective-permute-start.36 = (bf16[2048,128]{1,0:T(8,128)(2,1)S(1)}, bf16[2048,128]{1,0:T(8,128)(2,1)S(1)}, u32[]{:S(2)}, u32[]{:S(2)}) collective-permute-start(bf16[2048,128]{1,0:T(8,128)(2,1)S(1)} %get-tuple-element.72.refs_3_), channel_id=1, source_target_pairs={{0,8},{1,9},{2,10},{3,11},{4,12},{5,13},{6,14},{7,15},{8,16},{9,17... | collective-permute-start | bytes 1572872 | tf_op jit(solution)/shard_map/ppermute | solution.py:27
  64.8 16.6 %collective-permute-done.33.refs_1_ = bf16[2048,128]{1,0:T(8,128)(2,1)} collective-permute-done((bf16[2048,128]{1,0:T(8,128)(2,1)S(1)}, bf16[2048,128]{1,0:T(8,128)(2,1)}, u32[]{:S(2)}, u32[]{:S(2)}) %collective-permute-start.33) | collective-permute-done | bytes 524320 | tf_op jit(solution)/shard_map/ppermute | solution.py:27
  82.7 12.3 %collective-permute-start.21 = (bf16[2048,128]{1,0:T(8,128)(2,1)S(1)}, bf16[2048,128]{1,0:T(8,128)(2,1)S(1)}, u32[]{:S(2)}, u32[]{:S(2)}) collective-permute-start(bf16[2048,128]{1,0:T(8,128)(2,1)S(1)} %get-tuple-element.73.refs_3_), channel_id=1, source_target_pairs={{0,8},{1,9},{2,10},{3,11},{4,12},{5,13},{6,14},{7,15},{8,16},{9,17... | collective-permute-start | bytes 1572872 | tf_op jit(solution)/shard_map/ppermute | solution.py:27
  98.5 16.7 %collective-permute-done.18.refs_1_ = bf16[2048,128]{1,0:T(8,128)(2,1)} collective-permute-done((bf16[2048,128]{1,0:T(8,128)(2,1)S(1)}, bf16[2048,128]{1,0:T(8,128)(2,1)}, u32[]{:S(2)}, u32[]{:S(2)}) %collective-permute-start.18) | collective-permute-done | bytes 524320 | tf_op jit(solution)/shard_map/ppermute | solution.py:27
  119.0 12.3 %collective-permute-start.3 = (bf16[2048,128]{1,0:T(8,128)(2,1)S(1)}, bf16[2048,128]{1,0:T(8,128)(2,1)S(1)}, u32[]{:S(2)}, u32[]{:S(2)}) collective-permute-start(bf16[2048,128]{1,0:T(8,128)(2,1)S(1)} %get-tuple-element.70.refs_3_), channel_id=1, source_target_pairs={{0,8},{1,9},{2,10},{3,11},{4,12},{5,13},{6,14},{7,15},{8,16},{9,17... | collective-permute-start | bytes 1572872 | tf_op jit(solution)/shard_map/ppermute | solution.py:27
  164.8 65.3 %pick.7 = (bf16[2048,128]{1,0:T(8,128)(2,1)}, bf16[2048,128]{1,0:T(8,128)(2,1)}, bf16[2048,128]{1,0:T(8,128)(2,1)}, bf16[2048,128]{1,0:T(8,128)(2,1)}) custom-call(s32[4]{0:T(128)} %subtract_add_fusion.where_ref, bf16[2048,128]{1,0:T(8,128)(2,1)} %copy-done.22, bf16[2048,128]{1,0:T(8,128)(2,1)} %copy-done.19, ...), custom_call_target="tpu_custom_call" | custom-call | bytes 4194304 | tf_op jit(solution)/shard_map/pick/pallas_call | solution.py:80
  233.2 65.3 %pick.6 = (bf16[2048,128]{1,0:T(8,128)(2,1)}, bf16[2048,128]{1,0:T(8,128)(2,1)}, bf16[2048,128]{1,0:T(8,128)(2,1)}, bf16[2048,128]{1,0:T(8,128)(2,1)}) custom-call(s32[4]{0:T(128)} %subtract_add_fusion.where_ref, bf16[2048,128]{1,0:T(8,128)(2,1)} %collective-permute-done.34.refs_0_, bf16[2048,128]{1,0:T(8,128)(2,1)} %collective-permute-done.33.refs_1_, ...), custom_call_target="tpu_custom_call" | custom-call | bytes 4194304 | tf_op jit(solution)/shard_map/pick/pallas_call | solution.py:80
  301.0 11.7 %collective-permute-done.56.refs_3_ = bf16[2048,128]{1,0:T(8,128)(2,1)S(1)} collective-permute-done((bf16[2048,128]{1,0:T(8,128)(2,1)}, bf16[2048,128]{1,0:T(8,128)(2,1)S(1)}, u32[]{:S(2)}, u32[]{:S(2)}) %collective-permute-start.56) | collective-permute-done | bytes 524320 | tf_op jit(solution)/shard_map/ppermute | solution.py:27
  316.1 65.3 %pick.5 = (bf16[2048,128]{1,0:T(8,128)(2,1)}, bf16[2048,128]{1,0:T(8,128)(2,1)}, bf16[2048,128]{1,0:T(8,128)(2,1)}, bf16[2048,128]{1,0:T(8,128)(2,1)}) custom-call(s32[4]{0:T(128)} %subtract_add_fusion.where_ref, bf16[2048,128]{1,0:T(8,128)(2,1)} %collective-permute-done.19.refs_0_, bf16[2048,128]{1,0:T(8,128)(2,1)} %collective-permute-done.18.refs_1_, ...), custom_call_target="tpu_custom_call" | custom-call | bytes 4194304 | tf_op jit(solution)/shard_map/pick/pallas_call | solution.py:80
  384.4 12.4 %collective-permute-done.25.refs_2_ = bf16[2048,128]{1,0:T(8,128)(2,1)} collective-permute-done((bf16[2048,128]{1,0:T(8,128)(2,1)}, bf16[2048,128]{1,0:T(8,128)(2,1)}, u32[]{:S(2)}, u32[]{:S(2)}) %collective-permute-start.25) | collective-permute-done | bytes 524320 | tf_op jit(solution)/shard_map/ppermute | solution.py:27
  397.3 9.6 %collective-permute-done.26.refs_3_ = bf16[2048,128]{1,0:T(8,128)(2,1)} collective-permute-done((bf16[2048,128]{1,0:T(8,128)(2,1)}, bf16[2048,128]{1,0:T(8,128)(2,1)}, u32[]{:S(2)}, u32[]{:S(2)}) %collective-permute-start.26) | collective-permute-done | bytes 524320 | tf_op jit(solution)/shard_map/ppermute | solution.py:27
  408.1 65.3 %pick.4 = (bf16[2048,128]{1,0:T(8,128)(2,1)}, bf16[2048,128]{1,0:T(8,128)(2,1)}, bf16[2048,128]{1,0:T(8,128)(2,1)}, bf16[2048,128]{1,0:T(8,128)(2,1)}) custom-call(s32[4]{0:T(128)} %subtract_add_fusion.where_ref, bf16[2048,128]{1,0:T(8,128)(2,1)} %collective-permute-done.1.refs_0_, bf16[2048,128]{1,0:T(8,128)(2,1)} %copy-done.11, ...), custom_call_target="tpu_custom_call" | custom-call | bytes 4194304 | tf_op jit(solution)/shard_map/pick/pallas_call | solution.py:80
  477.7 19.1 %panel.7 = (f32[2,512,512]{2,1,0:T(8,128)}, bf16[2,512,512]{2,1,0:T(8,128)(2,1)}, f32[2,8,64,128]{3,2,1,0:T(8,128)}, bf16[2,8,64,128]{3,2,1,0:T(8,128)(2,1)}) custom-call(s32[3]{0:T(128)} %pad_add_fusion.where_ref, bf16[2048,4096]{1,0:T(8,128)(2,1)} %a_ref.7, bf16[2048,128]{1,0:T(8,128)(2,1)} %get-tuple-element.52.refs_0_, ...), custom_call_target="tpu_custom_call" | custom-call | flops 9663676416 | bytes 26214400 | tf_op jit(solution)/shard_map/panel/pallas_call | solution.py:187
  501.1 9.6 %collective-permute-done.44.refs_6_ = bf16[2048,128]{1,0:T(8,128)(2,1)S(1)} collective-permute-done((bf16[2048,128]{1,0:T(8,128)(2,1)}, bf16[2048,128]{1,0:T(8,128)(2,1)S(1)}, u32[]{:S(2)}, u32[]{:S(2)}) %collective-permute-start.44) | collective-permute-done | bytes 524320 | tf_op jit(solution)/shard_map/ppermute | solution.py:27
  512.3 9.8 %collective-permute-done.45.refs_7_ = bf16[2048,128]{1,0:T(8,128)(2,1)} collective-permute-done((bf16[2048,128]{1,0:T(8,128)(2,1)}, bf16[2048,128]{1,0:T(8,128)(2,1)}, u32[]{:S(2)}, u32[]{:S(2)}) %collective-permute-start.45) | collective-permute-done | bytes 524320 | tf_op jit(solution)/shard_map/ppermute | solution.py:27
  523.6 19.1 %panel.6 = (f32[2,512,512]{2,1,0:T(8,128)}, bf16[2,512,512]{2,1,0:T(8,128)(2,1)}, f32[2,8,64,128]{3,2,1,0:T(8,128)}, bf16[2,8,64,128]{3,2,1,0:T(8,128)(2,1)}) custom-call(s32[3]{0:T(128)} %pad_add_fusion.where_ref, bf16[2048,4096]{1,0:T(8,128)(2,1)} %a_ref.7, bf16[2048,128]{1,0:T(8,128)(2,1)} %get-tuple-element.46.refs_0_, bf16[2048,128]{1,0:T(8,128)(2,1)} %copy-done.27, ...), custom_call_target="tpu_custom_call" | custom-call | flops 9663676416 | bytes 26214400 | tf_op jit(solution)/shard_map/panel/pallas_call | solution.py:187
  546.9 8.8 %collective-permute-done.30.refs_7_ = bf16[2048,128]{1,0:T(8,128)(2,1)S(1)} collective-permute-done((bf16[2048,128]{1,0:T(8,128)(2,1)}, bf16[2048,128]{1,0:T(8,128)(2,1)S(1)}, u32[]{:S(2)}, u32[]{:S(2)}) %collective-permute-start.30) | collective-permute-done | bytes 524320 | tf_op jit(solution)/shard_map/ppermute | solution.py:27
  556.5 19.1 %panel.5 = (f32[2,512,512]{2,1,0:T(8,128)}, bf16[2,512,512]{2,1,0:T(8,128)(2,1)}, f32[2,8,64,128]{3,2,1,0:T(8,128)}, bf16[2,8,64,128]{3,2,1,0:T(8,128)(2,1)}) custom-call(s32[3]{0:T(128)} %pad_add_fusion.where_ref, bf16[2048,4096]{1,0:T(8,128)(2,1)} %a_ref.7, bf16[2048,128]{1,0:T(8,128)(2,1)} %get-tuple-element.40.refs_0_, ...), custom_call_target="tpu_custom_call" | custom-call | flops 9663676416 | bytes 26214400 | tf_op jit(solution)/shard_map/panel/pallas_call | solution.py:187
  578.3 11.2 %collective-permute-done.11.refs_6_ = bf16[2048,128]{1,0:T(8,128)(2,1)} collective-permute-done((bf16[2048,128]{1,0:T(8,128)(2,1)}, bf16[2048,128]{1,0:T(8,128)(2,1)}, u32[]{:S(2)}, u32[]{:S(2)}) %collective-permute-start.11) | collective-permute-done | bytes 524320 | tf_op jit(solution)/shard_map/ppermute | solution.py:27
  589.5 10.7 %collective-permute-done.12.refs_7_ = bf16[2048,128]{1,0:T(8,128)(2,1)} collective-permute-done((bf16[2048,128]{1,0:T(8,128)(2,1)}, bf16[2048,128]{1,0:T(8,128)(2,1)}, u32[]{:S(2)}, u32[]{:S(2)}) %collective-permute-start.12) | collective-permute-done | bytes 524320 | tf_op jit(solution)/shard_map/ppermute | solution.py:27
  600.2 19.2 %panel.4 = (f32[2,512,512]{2,1,0:T(8,128)}, bf16[2,512,512]{2,1,0:T(8,128)(2,1)}, f32[2,8,64,128]{3,2,1,0:T(8,128)}, bf16[2,8,64,128]{3,2,1,0:T(8,128)(2,1)}) custom-call(s32[3]{0:T(128)} %pad_add_fusion.where_ref, bf16[2048,4096]{1,0:T(8,128)(2,1)} %a_ref.7, bf16[2048,128]{1,0:T(8,128)(2,1)} %get-tuple-element.34.refs_0_, ...), custom_call_target="tpu_custom_call" | custom-call | flops 9663676416 | bytes 26214400 | tf_op jit(solution)/shard_map/panel/pallas_call | solution.py:187
  685.9 10.8 %collective-permute-start.82 = (f32[1,64,128]{2,1,0:T(8,128)S(1)}, f32[1,64,128]{2,1,0:T(8,128)S(1)}, u32[]{:S(2)}, u32[]{:S(2)}) collective-permute-start(f32[1,64,128]{2,1,0:T(8,128)S(1)} %slice.235), channel_id=1, source_target_pairs={{0,16},{1,17},{2,18},{3,19},{4,20},{5,21},{6,22},{7,23},{8,24},{9,... | collective-permute-start | bytes 98312 | tf_op jit(solution)/shard_map/ppermute | solution.py:27
  720.2 7.6 %collective-permute-done.62 = bf16[1,512,512]{2,1,0:T(8,128)(2,1)S(1)} collective-permute-done((bf16[1,512,512]{2,1,0:T(8,128)(2,1)S(1)}, bf16[1,512,512]{2,1,0:T(8,128)(2,1)S(1)}, u32[]{:S(2)}, u32[]{:S(2)}) %collective-permute-start.62) | collective-permute-done | bytes 524320 | tf_op jit(solution)/shard_map/ppermute | solution.py:27
  (283 shorter events, 211.0 us)
Async XLA Ops:
  9.6 51.8 %collective-permute-start.51 = (bf16[2048,128]{1,0:T(8,128)(2,1)S(1)}, bf16[2048,128]{1,0:T(8,128)(2,1)S(1)}, u32[]{:S(2)}, u32[]{:S(2)}) collective-permute-start(bf16[2048,128]{1,0:T(8,128)(2,1)S(1)} %get-tuple-element.71.refs_3_), channel_id=1, source_target_pairs={{0,8},{1,9},{2,10},{3,11},{4,12},{5,13},{6,14},{7,15},{8,16},{9,17... | collective-permute-start | bytes 1572872 | tf_op jit(solution)/shard_map/ppermute | solution.py:27
  21.0 60.4 %collective-permute-start.33 = (bf16[2048,128]{1,0:T(8,128)(2,1)S(1)}, bf16[2048,128]{1,0:T(8,128)(2,1)}, u32[]{:S(2)}, u32[]{:S(2)}) collective-permute-start(bf16[2048,128]{1,0:T(8,128)(2,1)S(1)} %get-tuple-element.72.refs_3_), channel_id=1, source_target_pairs={{16,0},{17,1},{18,2},{19,3},{20,4},{21,5},{22,6},{23,7},{24,8},{25... | collective-permute-start | bytes 1572872 | tf_op jit(solution)/shard_map/ppermute | solution.py:27
  37.9 57.2 %collective-permute-start.36 = (bf16[2048,128]{1,0:T(8,128)(2,1)S(1)}, bf16[2048,128]{1,0:T(8,128)(2,1)S(1)}, u32[]{:S(2)}, u32[]{:S(2)}) collective-permute-start(bf16[2048,128]{1,0:T(8,128)(2,1)S(1)} %get-tuple-element.72.refs_3_), channel_id=1, source_target_pairs={{0,8},{1,9},{2,10},{3,11},{4,12},{5,13},{6,14},{7,15},{8,16},{9,17... | collective-permute-start | bytes 1572872 | tf_op jit(solution)/shard_map/ppermute | solution.py:27
  116.5 184.5 %collective-permute-start.14 = (bf16[4,2048,128]{2,1,0:T(8,128)(2,1)S(1)}, bf16[4,2048,128]{2,1,0:T(8,128)(2,1)}, u32[]{:S(2)}, u32[]{:S(2)}) collective-permute-start(bf16[4,2048,128]{2,1,0:T(8,128)(2,1)S(1)} %bitcast_select_fusion.refs_8_), channel_id=1, source_target_pairs={{0,2},{1,3},{2,0},{3,1},{4,6},{5,7},{6,4},{7,5},{8,10},{9,11},{10,... | collective-permute-start | bytes 6291464 | tf_op jit(solution)/shard_map/ppermute | solution.py:27
  151.5 78.7 %collective-permute-start.38 = (bf16[2048,128]{1,0:T(8,128)(2,1)}, bf16[2048,128]{1,0:T(8,128)(2,1)}, u32[]{:S(2)}, u32[]{:S(2)}) collective-permute-start(bf16[2048,128]{1,0:T(8,128)(2,1)} %collective-permute-done.37.refs_5_), channel_id=1, source_target_pairs={{16,24},{17,25},{18,26},{19,27},{20,28},{21,29},{22,30},{23,31}} | collective-permute-start | bytes 1572872 | tf_op jit(solution)/shard_map/ppermute | solution.py:27
  152.9 78.7 %collective-permute-start.19 = (bf16[2048,128]{1,0:T(8,128)(2,1)}, bf16[2048,128]{1,0:T(8,128)(2,1)}, u32[]{:S(2)}, u32[]{:S(2)}) collective-permute-start(bf16[2048,128]{1,0:T(8,128)(2,1)} %collective-permute-done.18.refs_1_), channel_id=1, source_target_pairs={{8,0},{9,1},{10,2},{11,3},{12,4},{13,5},{14,6},{15,7}} | collective-permute-start | bytes 1572872 | tf_op jit(solution)/shard_map/ppermute | solution.py:27
  155.1 76.5 %collective-permute-start.23 = (bf16[2048,128]{1,0:T(8,128)(2,1)}, bf16[2048,128]{1,0:T(8,128)(2,1)}, u32[]{:S(2)}, u32[]{:S(2)}) collective-permute-start(bf16[2048,128]{1,0:T(8,128)(2,1)} %collective-permute-done.22.refs_5_), channel_id=1, source_target_pairs={{16,24},{17,25},{18,26},{19,27},{20,28},{21,29},{22,30},{23,31}} | collective-permute-start | bytes 1572872 | tf_op jit(solution)/shard_map/ppermute | solution.py:27
  163.5 135.1 %collective-permute-start.1 = (bf16[2048,128]{1,0:T(8,128)(2,1)}, bf16[2048,128]{1,0:T(8,128)(2,1)}, u32[]{:S(2)}, u32[]{:S(2)}) collective-permute-start(bf16[2048,128]{1,0:T(8,128)(2,1)} %copy-done.11), channel_id=1, source_target_pairs={{8,0},{9,1},{10,2},{11,3},{12,4},{13,5},{14,6},{15,7}} | collective-permute-start | bytes 1572872 | tf_op jit(solution)/shard_map/ppermute | solution.py:27
  230.2 68.8 %collective-permute-start.5 = (bf16[2048,128]{1,0:T(8,128)(2,1)}, bf16[2048,128]{1,0:T(8,128)(2,1)}, u32[]{:S(2)}, u32[]{:S(2)}) collective-permute-start(bf16[2048,128]{1,0:T(8,128)(2,1)} %copy-done.14), channel_id=1, source_target_pairs={{16,24},{17,25},{18,26},{19,27},{20,28},{21,29},{22,30},{23,31}} | collective-permute-start | bytes 1572872 | tf_op jit(solution)/shard_map/ppermute | solution.py:27
  231.6 68.8 %collective-permute-start.54 = (bf16[2048,128]{1,0:T(8,128)(2,1)}, bf16[2048,128]{1,0:T(8,128)(2,1)}, u32[]{:S(2)}, u32[]{:S(2)}) collective-permute-start(bf16[2048,128]{1,0:T(8,128)(2,1)} %get-tuple-element.53), channel_id=1, source_target_pairs={{0,1},{1,0},{2,3},{3,2},{4,5},{5,4},{6,7},{7,6},{8,9},{9,8},{10,11... | collective-permute-start | bytes 1572872 | tf_op jit(solution)/shard_map/ppermute | solution.py:27
  231.6 68.9 %collective-permute-start.55 = (bf16[2048,128]{1,0:T(8,128)(2,1)}, bf16[2048,128]{1,0:T(8,128)(2,1)}, u32[]{:S(2)}, u32[]{:S(2)}) collective-permute-start(bf16[2048,128]{1,0:T(8,128)(2,1)} %get-tuple-element.54), channel_id=1, source_target_pairs={{0,2},{1,3},{2,0},{3,1},{4,6},{5,7},{6,4},{7,5},{8,10},{9,11},{10,... | collective-permute-start | bytes 1572872 | tf_op jit(solution)/shard_map/ppermute | solution.py:27
  300.5 175.2 %collective-permute-start.13 = (bf16[4,2048,128]{2,1,0:T(8,128)(2,1)S(1)}, bf16[4,2048,128]{2,1,0:T(8,128)(2,1)}, u32[]{:S(2)}, u32[]{:S(2)}) collective-permute-start(bf16[4,2048,128]{2,1,0:T(8,128)(2,1)S(1)} %bitcast_select_fusion.refs_8_), channel_id=1, source_target_pairs={{0,1},{1,0},{2,3},{3,2},{4,5},{5,4},{6,7},{7,6},{8,9},{9,8},{10,11... | collective-permute-start | bytes 6291464 | tf_op jit(solution)/shard_map/ppermute | solution.py:27
  300.9 176.2 %collective-permute-start.15 = (bf16[4,2048,128]{2,1,0:T(8,128)(2,1)}, bf16[4,2048,128]{2,1,0:T(8,128)(2,1)}, u32[]{:S(2)}, u32[]{:S(2)}) collective-permute-start(bf16[4,2048,128]{2,1,0:T(8,128)(2,1)} %collective-permute-done.14.refs_10_), channel_id=1, source_target_pairs={{0,1},{1,0},{2,3},{3,2},{4,5},{5,4},{6,7},{7,6},{8,9},{9,8},{10,11... | collective-permute-start | bytes 6291464 | tf_op jit(solution)/shard_map/ppermute | solution.py:27
  312.8 68.7 %collective-permute-start.40 = (bf16[2048,128]{1,0:T(8,128)(2,1)}, bf16[2048,128]{1,0:T(8,128)(2,1)}, u32[]{:S(2)}, u32[]{:S(2)}) collective-permute-start(bf16[2048,128]{1,0:T(8,128)(2,1)} %get-tuple-element.48), channel_id=1, source_target_pairs={{0,2},{1,3},{2,0},{3,1},{4,6},{5,7},{6,4},{7,5},{8,10},{9,11},{10,... | collective-permute-start | bytes 1572872 | tf_op jit(solution)/shard_map/ppermute | solution.py:27
  313.3 68.4 %collective-permute-start.41 = (bf16[2048,128]{1,0:T(8,128)(2,1)}, bf16[2048,128]{1,0:T(8,128)(2,1)}, u32[]{:S(2)}, u32[]{:S(2)}) collective-permute-start(bf16[2048,128]{1,0:T(8,128)(2,1)} %get-tuple-element.49), channel_id=1, source_target_pairs={{0,3},{1,2},{2,1},{3,0},{4,7},{5,6},{6,5},{7,4},{8,11},{9,10},{10,... | collective-permute-start | bytes 1572872 | tf_op jit(solution)/shard_map/ppermute | solution.py:27
  314.6 68.1 %collective-permute-start.42 = (bf16[2048,128]{1,0:T(8,128)(2,1)}, bf16[2048,128]{1,0:T(8,128)(2,1)}, u32[]{:S(2)}, u32[]{:S(2)}) collective-permute-start(bf16[2048,128]{1,0:T(8,128)(2,1)} %get-tuple-element.46.refs_0_), channel_id=1, source_target_pairs={{0,4},{1,5},{2,6},{3,7},{4,0},{5,1},{6,2},{7,3},{8,12},{9,13},{10,... | collective-permute-start | bytes 1572872 | tf_op jit(solution)/shard_map/ppermute | solution.py:27
  383.8 89.6 %collective-permute-start.58 = (bf16[2048,128]{1,0:T(8,128)(2,1)}, bf16[2048,128]{1,0:T(8,128)(2,1)}, u32[]{:S(2)}, u32[]{:S(2)}) collective-permute-start(bf16[2048,128]{1,0:T(8,128)(2,1)} %collective-permute-done.54.refs_1_), channel_id=1, source_target_pairs={{0,4},{1,5},{2,6},{3,7},{4,0},{5,1},{6,2},{7,3},{8,12},{9,13},{10,... | collective-permute-start | bytes 1572872 | tf_op jit(solution)/shard_map/ppermute | solution.py:27
  396.8 78.2 %collective-permute-start.59 = (bf16[2048,128]{1,0:T(8,128)(2,1)}, bf16[2048,128]{1,0:T(8,128)(2,1)}, u32[]{:S(2)}, u32[]{:S(2)}) collective-permute-start(bf16[2048,128]{1,0:T(8,128)(2,1)} %collective-permute-done.55.refs_2_), channel_id=1, source_target_pairs={{0,4},{1,5},{2,6},{3,7},{4,0},{5,1},{6,2},{7,3},{8,12},{9,13},{10,... | collective-permute-start | bytes 1572872 | tf_op jit(solution)/shard_map/ppermute | solution.py:27
  406.9 68.2 %collective-permute-start.60 = (bf16[2048,128]{1,0:T(8,128)(2,1)}, bf16[2048,128]{1,0:T(8,128)(2,1)}, u32[]{:S(2)}, u32[]{:S(2)}) collective-permute-start(bf16[2048,128]{1,0:T(8,128)(2,1)} %copy-done.28), channel_id=1, source_target_pairs={{0,4},{1,5},{2,6},{3,7},{4,0},{5,1},{6,2},{7,3},{8,12},{9,13},{10,... | collective-permute-start | bytes 1572872 | tf_op jit(solution)/shard_map/ppermute | solution.py:27
  545.4 54.8 %collective-permute-start.12 = (bf16[2048,128]{1,0:T(8,128)(2,1)}, bf16[2048,128]{1,0:T(8,128)(2,1)}, u32[]{:S(2)}, u32[]{:S(2)}) collective-permute-start(bf16[2048,128]{1,0:T(8,128)(2,1)} %collective-permute-done.8.refs_3_), channel_id=1, source_target_pairs={{0,4},{1,5},{2,6},{3,7},{4,0},{5,1},{6,2},{7,3},{8,12},{9,13},{10,... | collective-permute-start | bytes 1572872 | tf_op jit(solution)/shard_map/ppermute | solution.py:27
  556.5 157.2 %collective-permute-start.61 = (bf16[2,512,512]{2,1,0:T(8,128)(2,1)}, bf16[2,512,512]{2,1,0:T(8,128)(2,1)S(1)}, u32[]{:S(2)}, u32[]{:S(2)}) collective-permute-start(bf16[2,512,512]{2,1,0:T(8,128)(2,1)} %get-tuple-element.57), channel_id=1, source_target_pairs={{0,1},{1,0},{2,3},{3,2},{4,5},{5,4},{6,7},{7,6},{8,9},{9,8},{10,11... | collective-permute-start | bytes 3145736 | tf_op jit(solution)/shard_map/ppermute | solution.py:27
  575.7 139.8 %collective-permute-start.46 = (bf16[2,512,512]{2,1,0:T(8,128)(2,1)}, bf16[2,512,512]{2,1,0:T(8,128)(2,1)S(1)}, u32[]{:S(2)}, u32[]{:S(2)}) collective-permute-start(bf16[2,512,512]{2,1,0:T(8,128)(2,1)} %get-tuple-element.51), channel_id=1, source_target_pairs={{0,1},{1,0},{2,3},{3,2},{4,5},{5,4},{6,7},{7,6},{8,9},{9,8},{10,11... | collective-permute-start | bytes 3145736 | tf_op jit(solution)/shard_map/ppermute | solution.py:27
  578.3 138.7 %collective-permute-start.31 = (bf16[2,512,512]{2,1,0:T(8,128)(2,1)}, bf16[2,512,512]{2,1,0:T(8,128)(2,1)S(1)}, u32[]{:S(2)}, u32[]{:S(2)}) collective-permute-start(bf16[2,512,512]{2,1,0:T(8,128)(2,1)} %get-tuple-element.45), channel_id=1, source_target_pairs={{0,1},{1,0},{2,3},{3,2},{4,5},{5,4},{6,7},{7,6},{8,9},{9,8},{10,11... | collective-permute-start | bytes 3145736 | tf_op jit(solution)/shard_map/ppermute | solution.py:27
  622.6 96.0 %collective-permute-start.16 = (bf16[2,512,512]{2,1,0:T(8,128)(2,1)S(1)}, bf16[2,512,512]{2,1,0:T(8,128)(2,1)S(1)}, u32[]{:S(2)}, u32[]{:S(2)}) collective-permute-start(bf16[2,512,512]{2,1,0:T(8,128)(2,1)S(1)} %copy-done.25), channel_id=1, source_target_pairs={{0,1},{1,0},{2,3},{3,2},{4,5},{5,4},{6,7},{7,6},{8,9},{9,8},{10,11... | collective-permute-start | bytes 3145736 | tf_op jit(solution)/shard_map/ppermute | solution.py:27
  (95 other events, 3239.0 us)

commit v2 on v1

--- a/solution.py
+++ b/solution.py
@@ -6,6 +6,7 @@
 from jax.experimental import pallas as pl
 from jax.experimental.pallas import tpu as pltpu
 from jax.sharding import PartitionSpec as P
+
 
 TILE = 128
 AXES = ("row", "col")
@@ -43,18 +44,22 @@
         return self.move(value, target)
 
 
-def line_gather(grid, own):
-    n = grid.cols
+def line_start(grid, own):
     values = {0: own}
-    for sign in (1, -1):
-        for far in range(1, n):
-            if far <= 2:
+    for far in (2, 1):
+        for sign in (1, -1):
+            if far < grid.cols:
                 values[sign * far] = grid.group_shift(own, sign * far)
-            else:
-                values[sign * far] = grid.group_shift(
-                    values[sign * (far - 1)], sign, held=sign * (far - 1)
-                )
-    return [values[delta] for delta in range(-(n - 1), n)]
+    return values
+
+
+def line_finish(grid, values):
+    for far in range(3, grid.cols):
+        for sign in (1, -1):
+            values[sign * far] = grid.group_shift(
+                values[sign * (far - 1)], sign, held=sign * (far - 1)
+            )
+    return [values[delta] for delta in range(1 - grid.cols, grid.cols)]
 
 
 def pick_kernel(n, where_ref, *refs):
@@ -83,7 +88,7 @@
             num_scalar_prefetch=1,
             grid=(1,),
             in_specs=[pl.BlockSpec(memory_space=pl.ANY)] * (2 * n - 1),
-            out_specs=[pl.BlockSpec(memory_space=pl.ANY)] * n,
+            out_specs=[pl.BlockSpec(shape, lambda g, w: (0,) * len(shape))] * n,
             scratch_shapes=[pltpu.SemaphoreType.DMA((n,))],
         ),
         out_shape=[jax.ShapeDtypeStruct(shape, values[0].dtype)] * n,
@@ -150,7 +155,7 @@
 def panel(grid, where, inverse_tiles, pieces, left, supers):
     n, per, rows_all = grid.cols, grid.per, grid.rows
     col, offset, row = where[0], where[1], where[2]
-    depth, width = pieces[0][0].shape[-2:]
+    _, width = pieces[0][0].shape[-2:]
     rows_blk, cols_blk = inverse_tiles.shape
     share = rows_blk // n
     panel_width = n * width
@@ -219,23 +224,35 @@
     )(where, inverse_tiles, *[value for line in pieces for value in line], *left)
 
 
-def halve_cols(grid, keep, send):
+def reduce_panel(grid, keep, send, out):
     bit = 1
     while True:
-        keep = keep + grid.col_swap(send, bit).astype(jnp.float32)
+        moved = grid.col_swap(send, bit)
+        yield
+        keep = keep + moved.astype(jnp.float32)
         bit *= 2
         if bit >= grid.cols:
-            return keep[0]
+            break
         send, keep = keep[1::2].astype(jnp.bfloat16), keep[0::2]
-
-
-def halve_rows(grid, value):
+    out.append(keep[0])
+
+
+def reduce_diag(grid, keep, send, out):
+    yield from reduce_panel(grid, keep, send, out)
+    value = out.pop()
     bit = 1
     while bit < grid.rows:
-        send, value = value[1::2], value[0::2]
-        value = value + grid.row_swap(send, bit)
+        moved = grid.row_swap(value[1::2], bit)
+        yield
+        value = value[0::2] + moved
         bit *= 2
-    return value[0]
+    out.append(value[0])
+
+
+def advance(running):
+    for steps in list(running):
+        if next(steps, running) is running:
+            running.remove(steps)
 
 
 def per_device(inverse_tiles, factor, inverse_diag, tile_list, tile_count):
@@ -263,29 +280,87 @@
     where_pick = group - (col ^ jnp.arange(grid.cols, dtype=jnp.int32)) + grid.cols - 1
     where_panel = jnp.stack([col, offset, row]).astype(jnp.int32)
 
-    left = {0: masked}
+    def rows_of(chunk):
+        return masked[chunk[0]] if len(chunk) == 1 else masked[chunk[0] : chunk[-1] + 1]
+
+    last = len(chunks) - 1
+    jobs = [(at, 0) for at in range(len(chunks))]
+    if last:
+        jobs += [(last, t) for t in range(1, grid.per)]
+    lines, pieces, left = {}, {}, {0: masked}
+    panels, diags = [[] for _ in chunks], [[] for _ in chunks]
+    running = []
+
+    def start(k):
+        at, t = jobs[k]
+        lines[k] = line_start(grid, early[t] if t else rows_of(chunks[at]))
+
+    def spread(k):
+        picked = pick(grid, lines.pop(k), where_pick)
+        pieces[k] = [picked[0]] + [grid.col_swap(picked[d], d) for d in range(1, grid.cols)]
+
+    def across(k, some):
+        at, t = jobs[k]
+        if last and at == last:
+            return
+        for t in range(1, grid.per):
+            for d in some:
+                pieces[k, t, d] = grid.row_swap(pieces[k][d], t)
+
+    def multiply(at):
+        if last and at == last:
+            full = [pieces[k] for k in range(last, len(jobs))]
+        else:
+            full = [pieces[at]] + [
+                [pieces[at, t, d] for d in range(grid.cols)] for t in range(1, grid.per)
+            ]
+        keep, send, diag_keep, diag_send = panel(
+            grid, where_panel, inverse_tiles, full, [left[d] for d in range(grid.cols)], chunks[at]
+        )
+        running.append(reduce_diag(grid, diag_keep, diag_send, diags[at]))
+        running.append(reduce_panel(grid, keep, send, panels[at]))
+
+    start(0)
     bit = grid.cols // 2
-    while bit:
-        for d in list(left):
-            left[d | bit] = grid.col_swap(left[d], bit)
-        bit //= 2
-    left = [left[d] for d in range(grid.cols)]
-
-    panels, diags = [], []
-    for chunk in chunks:
-        own = masked[chunk[0]] if len(chunk) == 1 else masked[chunk[0] : chunk[-1] + 1]
-        picked = pick(grid, line_gather(grid, own), where_pick)
-        line = [picked[0]] + [grid.col_swap(picked[d], d) for d in range(1, grid.cols)]
-        pieces = [line] + [
-            [grid.row_swap(value, t) for value in line] for t in range(1, grid.per)
-        ]
-        keep, send, diag_keep, diag_send = panel(
-            grid, where_panel, inverse_tiles, pieces, left, chunk
-        )
-        total = halve_cols(grid, keep, send)
-        diag = halve_rows(grid, halve_cols(grid, diag_keep, diag_send))
-        panels.append(total.reshape(len(chunk), share, -1))
-        diags.append(diag.reshape(len(chunk), -1, width))
+    left[bit] = grid.col_swap(masked, bit)
+    early = {}
+    if last:
+        early = {t: grid.row_swap(rows_of(chunks[last]), t) for t in range(1, grid.per)}
+    bit //= 2
+    near = [d for d in range(grid.cols) if d < 2]
+    far = [d for d in range(grid.cols) if d >= 2]
+    for k in range(len(jobs)):
+        lines[k] = line_finish(grid, lines[k])
+        if k + 1 < len(jobs):
+            start(k + 1)
+        if k:
+            across(k - 1, far)
+        advance(running)
+        if k == len(jobs) - 1 and k >= 3:
+            multiply(k - 3)
+        spread(k)
+        across(k, near)
+        advance(running)
+        if k == 0:
+            while bit:
+                for d in list(left):
+                    left[d | bit] = grid.col_swap(left[d], bit)
+                bit //= 2
+        if 2 <= k < len(jobs) - 2 or (k >= 2 and k == len(jobs) - 2 and False):
+            multiply(k - 2)
+            advance(running)
+    across(len(jobs) - 1, far)
+    done = {at for at in range(len(chunks)) if 2 <= at + 2 < len(jobs) - 2}
+    if len(jobs) >= 4:
+        done.add(len(jobs) - 4)
+    for at in range(len(chunks)):
+        if at not in done:
+            multiply(at)
+            advance(running)
+    while running:
+        advance(running)
+    panels = [value[0].reshape(len(chunk), share, -1) for value, chunk in zip(panels, chunks)]
+    diags = [value[0].reshape(len(chunk), -1, width) for value, chunk in zip(diags, chunks)]
 
     summed = jnp.concatenate(panels, axis=0)
     share_live = lax.dynamic_slice_in_dim(live, col * share, share, 1).astype(jnp.float32)
@@ -296,6 +371,7 @@
 
 def solution(mesh):
     placed = (P("row", "col"), P("row", None, "col"), P(None, "row", "col"), P(), P())
+
     return jax.shard_map(
         per_device,
         mesh=mesh,

time: 749 us -> 547 us (0.73)
  Pallas kernels: 338 us -> 94.7 us
  waiting for transfers between devices: 229 us -> 252 us
  starting transfers between devices: 161 us -> 178 us
    pallas_call x4 -> x5, Pallas kernels: 261 us -> 17.9 us  [pick(): pl.pallas_call(functools.partial(pick_kernel, n), grid_spec=pltpu.Prefetc...]
    ppermute x83 -> x89, waiting for transfers between devices: 229 us -> 252 us  [move(): return lax.ppermute(value, AXES, pairs)]
    ppermute x83 -> x89, starting transfers between devices: 161 us -> 178 us  [move(): return lax.ppermute(value, AXES, pairs)]
  transfers between devices with their start and end apart: 83 -> 89, of which waited for: 40 -> 45; matrix products, arithmetic and copies ran while one was open for 1% -> 1% of each run, Pallas kernels for 45% -> 17%
where the time goes in v2:
time: 547 us; the launch traced here: 546 us
  waiting for transfers between devices  252 us (46%)
  starting transfers between devices  178 us (33%)
  Pallas kernels  94.7 us (17%)
  other arithmetic  13.4 us (2%)
  local copies, waits for them, and re-layouts  5.87 us (1%)
    ppermute x89, waiting for transfers between devices, move(): return lax.ppermute(value, AXES, pairs)  252 us
    ppermute x89, starting transfers between devices, move(): return lax.ppermute(value, AXES, pairs)  178 us
    pallas_call x4, Pallas kernels, panel(): pl.pallas_call(functools.partial(panel_kernel, n, per, rows_all), grid_sp...  76.8 us
    pallas_call x5, Pallas kernels, pick(): pl.pallas_call(functools.partial(pick_kernel, n), grid_spec=pltpu.Prefetc...  17.9 us
  transfers between devices with their start and end apart: 89, of which 45 were waited for; matrix products, arithmetic and copies ran while one was open for 1% of the time, Pallas kernels for 17%

profile of v2, /device:TPU:0, one launch (start us, length us, event | category | flops | bytes accessed | tf_op | source)
XLA Modules:
  0.0 545.9 jit_solution(10953690472514314517)
XLA Ops:
  9.6 6.4 %collective-permute-start.51 = (bf16[2048,128]{1,0:T(8,128)(2,1)S(1)}, bf16[2048,128]{1,0:T(8,128)(2,1)}, u32[]{:S(2)}, u32[]{:S(2)}) collective-permute-start(bf16[2048,128]{1,0:T(8,128)(2,1)S(1)} %get-tuple-element.79.refs_3_), channel_id=1, source_target_pairs={{0,8},{1,9},{2,10},{3,11},{4,12},{5,13},{6,14},{7,15},{8,16},{9,17... | collective-permute-start | bytes 1572872 | tf_op jit(solution)/shard_map/ppermute | solution.py:28
  22.8 13.8 %collective-permute-done.48.refs_1_ = bf16[2048,128]{1,0:T(8,128)(2,1)S(1)} collective-permute-done((bf16[2048,128]{1,0:T(8,128)(2,1)S(1)}, bf16[2048,128]{1,0:T(8,128)(2,1)S(1)}, u32[]{:S(2)}, u32[]{:S(2)}) %collective-permute-start.48) | collective-permute-done | bytes 524320 | tf_op jit(solution)/shard_map/ppermute | solution.py:28
  39.2 24.1 %collective-permute-start.36 = (bf16[2048,128]{1,0:T(8,128)(2,1)S(1)}, bf16[2048,128]{1,0:T(8,128)(2,1)S(1)}, u32[]{:S(2)}, u32[]{:S(2)}) collective-permute-start(bf16[2048,128]{1,0:T(8,128)(2,1)S(1)} %get-tuple-element.80.refs_3_), channel_id=1, source_target_pairs={{0,8},{1,9},{2,10},{3,11},{4,12},{5,13},{6,14},{7,15},{8,16},{9,17... | collective-permute-start | bytes 1572872 | tf_op jit(solution)/shard_map/ppermute | solution.py:28
  71.5 9.1 %collective-permute-done.35.refs_2_ = bf16[2048,128]{1,0:T(8,128)(2,1)S(1)} collective-permute-done((bf16[2048,128]{1,0:T(8,128)(2,1)S(1)}, bf16[2048,128]{1,0:T(8,128)(2,1)S(1)}, u32[]{:S(2)}, u32[]{:S(2)}) %collective-permute-start.35) | collective-permute-done | bytes 524320 | tf_op jit(solution)/shard_map/ppermute | solution.py:28
  80.6 15.3 %collective-permute-start.21 = (bf16[2048,128]{1,0:T(8,128)(2,1)S(1)}, bf16[2048,128]{1,0:T(8,128)(2,1)}, u32[]{:S(2)}, u32[]{:S(2)}) collective-permute-start(bf16[2048,128]{1,0:T(8,128)(2,1)S(1)} %get-tuple-element.81.refs_3_), channel_id=1, source_target_pairs={{0,8},{1,9},{2,10},{3,11},{4,12},{5,13},{6,14},{7,15},{8,16},{9,17... | collective-permute-start | bytes 1572872 | tf_op jit(solution)/shard_map/ppermute | solution.py:28
  99.3 15.9 %collective-permute-done.18.refs_1_ = bf16[2048,128]{1,0:T(8,128)(2,1)} collective-permute-done((bf16[2048,128]{1,0:T(8,128)(2,1)S(1)}, bf16[2048,128]{1,0:T(8,128)(2,1)}, u32[]{:S(2)}, u32[]{:S(2)}) %collective-permute-start.18) | collective-permute-done | bytes 524320 | tf_op jit(solution)/shard_map/ppermute | solution.py:28
  116.5 12.4 %collective-permute-start.3 = (bf16[2048,128]{1,0:T(8,128)(2,1)S(1)}, bf16[2048,128]{1,0:T(8,128)(2,1)S(1)}, u32[]{:S(2)}, u32[]{:S(2)}) collective-permute-start(bf16[2048,128]{1,0:T(8,128)(2,1)S(1)} %get-tuple-element.78.refs_3_), channel_id=1, source_target_pairs={{0,8},{1,9},{2,10},{3,11},{4,12},{5,13},{6,14},{7,15},{8,16},{9,17... | collective-permute-start | bytes 1572872 | tf_op jit(solution)/shard_map/ppermute | solution.py:28
  131.5 6.1 %collective-permute-done.refs_1_ = bf16[2048,128]{1,0:T(8,128)(2,1)} collective-permute-done((bf16[2048,128]{1,0:T(8,128)(2,1)S(1)}, bf16[2048,128]{1,0:T(8,128)(2,1)}, u32[]{:S(2)}, u32[]{:S(2)}) %collective-permute-start) | collective-permute-done | bytes 524320 | tf_op jit(solution)/shard_map/ppermute | solution.py:28
  155.5 13.1 %collective-permute-start.61 = (bf16[2048,128]{1,0:T(8,128)(2,1)S(1)}, bf16[2048,128]{1,0:T(8,128)(2,1)S(1)}, u32[]{:S(2)}, u32[]{:S(2)}) collective-permute-start(bf16[2048,128]{1,0:T(8,128)(2,1)S(1)} %collective-permute-done.57.refs_3_), channel_id=1, source_target_pairs={{0,8},{1,9},{2,10},{3,11},{4,12},{5,13},{6,14},{7,15},{8,16},{9,17... | collective-permute-start | bytes 1572872 | tf_op jit(solution)/shard_map/ppermute | solution.py:28
  174.7 8.1 %collective-permute-done.60.refs_2_ = bf16[2048,128]{1,0:T(8,128)(2,1)S(1)} collective-permute-done((bf16[2048,128]{1,0:T(8,128)(2,1)S(1)}, bf16[2048,128]{1,0:T(8,128)(2,1)S(1)}, u32[]{:S(2)}, u32[]{:S(2)}) %collective-permute-start.60) | collective-permute-done | bytes 524320 | tf_op jit(solution)/shard_map/ppermute | solution.py:28
  201.8 6.3 %collective-permute-done.19.refs_0_ = bf16[2048,128]{1,0:T(8,128)(2,1)} collective-permute-done((bf16[2048,128]{1,0:T(8,128)(2,1)}, bf16[2048,128]{1,0:T(8,128)(2,1)}, u32[]{:S(2)}, u32[]{:S(2)}) %collective-permute-start.19) | collective-permute-done | bytes 524320 | tf_op jit(solution)/shard_map/ppermute | solution.py:28
  224.4 10.0 %collective-permute-done.56.refs_3_ = bf16[2048,128]{1,0:T(8,128)(2,1)} collective-permute-done((bf16[2048,128]{1,0:T(8,128)(2,1)}, bf16[2048,128]{1,0:T(8,128)(2,1)}, u32[]{:S(2)}, u32[]{:S(2)}) %collective-permute-start.56) | collective-permute-done | bytes 524320 | tf_op jit(solution)/shard_map/ppermute | solution.py:28
  243.7 7.5 %collective-permute-done.40.refs_2_ = bf16[2048,128]{1,0:T(8,128)(2,1)} collective-permute-done((bf16[2048,128]{1,0:T(8,128)(2,1)}, bf16[2048,128]{1,0:T(8,128)(2,1)}, u32[]{:S(2)}, u32[]{:S(2)}) %collective-permute-start.40) | collective-permute-done | bytes 524320 | tf_op jit(solution)/shard_map/ppermute | solution.py:28
  251.2 10.6 %collective-permute-done.41.refs_3_ = bf16[2048,128]{1,0:T(8,128)(2,1)} collective-permute-done((bf16[2048,128]{1,0:T(8,128)(2,1)}, bf16[2048,128]{1,0:T(8,128)(2,1)}, u32[]{:S(2)}, u32[]{:S(2)}) %collective-permute-start.41) | collective-permute-done | bytes 524320 | tf_op jit(solution)/shard_map/ppermute | solution.py:28
  265.3 11.7 %collective-permute-done.25.refs_2_ = bf16[2048,128]{1,0:T(8,128)(2,1)} collective-permute-done((bf16[2048,128]{1,0:T(8,128)(2,1)}, bf16[2048,128]{1,0:T(8,128)(2,1)}, u32[]{:S(2)}, u32[]{:S(2)}) %collective-permute-start.25) | collective-permute-done | bytes 524320 | tf_op jit(solution)/shard_map/ppermute | solution.py:28
  278.7 7.8 %collective-permute-done.26.refs_3_ = bf16[2048,128]{1,0:T(8,128)(2,1)} collective-permute-done((bf16[2048,128]{1,0:T(8,128)(2,1)}, bf16[2048,128]{1,0:T(8,128)(2,1)}, u32[]{:S(2)}, u32[]{:S(2)}) %collective-permute-start.26) | collective-permute-done | bytes 524320 | tf_op jit(solution)/shard_map/ppermute | solution.py:28
  303.4 19.3 %panel.6 = (f32[2,512,512]{2,1,0:T(8,128)}, bf16[2,512,512]{2,1,0:T(8,128)(2,1)}, f32[2,8,64,128]{3,2,1,0:T(8,128)}, bf16[2,8,64,128]{3,2,1,0:T(8,128)(2,1)}) custom-call(s32[3]{0:T(128)} %pad_add_fusion.where_ref, bf16[2048,4096]{1,0:T(8,128)(2,1)} %a_ref.7, bf16[2048,128]{1,0:T(8,128)(2,1)} %get-tuple-element.50.refs_0_, ...), custom_call_target="tpu_custom_call" | custom-call | flops 9663676416 | bytes 26214400 | tf_op jit(solution)/shard_map/panel/pallas_call | solution.py:192
  328.6 19.3 %panel.7 = (f32[2,512,512]{2,1,0:T(8,128)}, bf16[2,512,512]{2,1,0:T(8,128)(2,1)}, f32[2,8,64,128]{3,2,1,0:T(8,128)}, bf16[2,8,64,128]{3,2,1,0:T(8,128)(2,1)}) custom-call(s32[3]{0:T(128)} %pad_add_fusion.where_ref, bf16[2048,4096]{1,0:T(8,128)(2,1)} %a_ref.7, bf16[2048,128]{1,0:T(8,128)(2,1)} %get-tuple-element.56.refs_0_, ...), custom_call_target="tpu_custom_call" | custom-call | flops 9663676416 | bytes 26214400 | tf_op jit(solution)/shard_map/panel/pallas_call | solution.py:192
  352.9 9.2 %collective-permute-done.30.refs_7_ = bf16[2048,128]{1,0:T(8,128)(2,1)} collective-permute-done((bf16[2048,128]{1,0:T(8,128)(2,1)}, bf16[2048,128]{1,0:T(8,128)(2,1)}, u32[]{:S(2)}, u32[]{:S(2)}) %collective-permute-start.30) | collective-permute-done | bytes 524320 | tf_op jit(solution)/shard_map/ppermute | solution.py:28
  362.1 19.1 %panel.5 = (f32[2,512,512]{2,1,0:T(8,128)}, bf16[2,512,512]{2,1,0:T(8,128)(2,1)}, f32[2,8,64,128]{3,2,1,0:T(8,128)}, bf16[2,8,64,128]{3,2,1,0:T(8,128)(2,1)}) custom-call(s32[3]{0:T(128)} %pad_add_fusion.where_ref, bf16[2048,4096]{1,0:T(8,128)(2,1)} %a_ref.7, bf16[2048,128]{1,0:T(8,128)(2,1)} %get-tuple-element.44.refs_0_, ...), custom_call_target="tpu_custom_call" | custom-call | flops 9663676416 | bytes 26214400 | tf_op jit(solution)/shard_map/panel/pallas_call | solution.py:192
  384.6 11.2 %collective-permute-done.11.refs_6_ = bf16[2048,128]{1,0:T(8,128)(2,1)} collective-permute-done((bf16[2048,128]{1,0:T(8,128)(2,1)}, bf16[2048,128]{1,0:T(8,128)(2,1)}, u32[]{:S(2)}, u32[]{:S(2)}) %collective-permute-start.11) | collective-permute-done | bytes 524320 | tf_op jit(solution)/shard_map/ppermute | solution.py:28
  395.8 11.0 %collective-permute-done.12.refs_7_ = bf16[2048,128]{1,0:T(8,128)(2,1)} collective-permute-done((bf16[2048,128]{1,0:T(8,128)(2,1)}, bf16[2048,128]{1,0:T(8,128)(2,1)}, u32[]{:S(2)}, u32[]{:S(2)}) %collective-permute-start.12) | collective-permute-done | bytes 524320 | tf_op jit(solution)/shard_map/ppermute | solution.py:28
  406.9 19.1 %panel.4 = (f32[2,512,512]{2,1,0:T(8,128)}, bf16[2,512,512]{2,1,0:T(8,128)(2,1)}, f32[2,8,64,128]{3,2,1,0:T(8,128)}, bf16[2,8,64,128]{3,2,1,0:T(8,128)(2,1)}) custom-call(s32[3]{0:T(128)} %pad_add_fusion.where_ref, bf16[2048,4096]{1,0:T(8,128)(2,1)} %a_ref.7, bf16[2048,128]{1,0:T(8,128)(2,1)} %get-tuple-element.38.refs_0_, bf16[2048,128]{1,0:T(8,128)(2,1)} %copy-done.33, ...), custom_call_target="tpu_custom_call" | custom-call | flops 9663676416 | bytes 26214400 | tf_op jit(solution)/shard_map/panel/pallas_call | solution.py:192
  517.1 8.1 %collective-permute-done.68 = bf16[1,512,512]{2,1,0:T(8,128)(2,1)S(1)} collective-permute-done((bf16[1,512,512]{2,1,0:T(8,128)(2,1)S(1)}, bf16[1,512,512]{2,1,0:T(8,128)(2,1)S(1)}, u32[]{:S(2)}, u32[]{:S(2)}) %collective-permute-start.68) | collective-permute-done | bytes 524320 | tf_op jit(solution)/shard_map/ppermute | solution.py:28
  (304 shorter events, 249.5 us)
Async XLA Ops:
  16.0 47.3 %collective-permute-start.52 = (bf16[2048,128]{1,0:T(8,128)(2,1)S(1)}, bf16[2048,128]{1,0:T(8,128)(2,1)S(1)}, u32[]{:S(2)}, u32[]{:S(2)}) collective-permute-start(bf16[2048,128]{1,0:T(8,128)(2,1)S(1)} %get-tuple-element.79.refs_3_), channel_id=1, source_target_pairs={{0,16},{1,17},{2,18},{3,19},{4,20},{5,21},{6,22},{7,23},{8,24},{9,... | collective-permute-start | bytes 1572872 | tf_op jit(solution)/shard_map/ppermute | solution.py:28
  20.2 47.2 %collective-permute-start.57 = (bf16[2048,128]{1,0:T(8,128)(2,1)S(1)}, bf16[2048,128]{1,0:T(8,128)(2,1)S(1)}, u32[]{:S(2)}, u32[]{:S(2)}) collective-permute-start(bf16[2048,128]{1,0:T(8,128)(2,1)S(1)} %get-tuple-element.79.refs_3_), channel_id=1, source_target_pairs={{0,4},{1,5},{2,6},{3,7},{4,0},{5,1},{6,2},{7,3},{8,12},{9,13},{10,... | collective-permute-start | bytes 1572872 | tf_op jit(solution)/shard_map/ppermute | solution.py:28
  36.6 33.6 %collective-permute-start.33 = (bf16[2048,128]{1,0:T(8,128)(2,1)S(1)}, bf16[2048,128]{1,0:T(8,128)(2,1)S(1)}, u32[]{:S(2)}, u32[]{:S(2)}) collective-permute-start(bf16[2048,128]{1,0:T(8,128)(2,1)S(1)} %get-tuple-element.80.refs_3_), channel_id=1, source_target_pairs={{16,0},{17,1},{18,2},{19,3},{20,4},{21,5},{22,6},{23,7},{24,8},{25... | collective-permute-start | bytes 1572872 | tf_op jit(solution)/shard_map/ppermute | solution.py:28
  37.9 42.7 %collective-permute-start.35 = (bf16[2048,128]{1,0:T(8,128)(2,1)S(1)}, bf16[2048,128]{1,0:T(8,128)(2,1)S(1)}, u32[]{:S(2)}, u32[]{:S(2)}) collective-permute-start(bf16[2048,128]{1,0:T(8,128)(2,1)S(1)} %get-tuple-element.80.refs_3_), channel_id=1, source_target_pairs={{8,0},{9,1},{10,2},{11,3},{12,4},{13,5},{14,6},{15,7},{16,8},{17,9... | collective-permute-start | bytes 1572872 | tf_op jit(solution)/shard_map/ppermute | solution.py:28
  39.2 56.7 %collective-permute-start.36 = (bf16[2048,128]{1,0:T(8,128)(2,1)S(1)}, bf16[2048,128]{1,0:T(8,128)(2,1)S(1)}, u32[]{:S(2)}, u32[]{:S(2)}) collective-permute-start(bf16[2048,128]{1,0:T(8,128)(2,1)S(1)} %get-tuple-element.80.refs_3_), channel_id=1, source_target_pairs={{0,8},{1,9},{2,10},{3,11},{4,12},{5,13},{6,14},{7,15},{8,16},{9,17... | collective-permute-start | bytes 1572872 | tf_op jit(solution)/shard_map/ppermute | solution.py:28
  63.3 34.7 %collective-permute-start.37 = (bf16[2048,128]{1,0:T(8,128)(2,1)S(1)}, bf16[2048,128]{1,0:T(8,128)(2,1)}, u32[]{:S(2)}, u32[]{:S(2)}) collective-permute-start(bf16[2048,128]{1,0:T(8,128)(2,1)S(1)} %get-tuple-element.80.refs_3_), channel_id=1, source_target_pairs={{0,16},{1,17},{2,18},{3,19},{4,20},{5,21},{6,22},{7,23},{8,24},{9,... | collective-permute-start | bytes 1572872 | tf_op jit(solution)/shard_map/ppermute | solution.py:28
  67.5 47.7 %collective-permute-start.18 = (bf16[2048,128]{1,0:T(8,128)(2,1)S(1)}, bf16[2048,128]{1,0:T(8,128)(2,1)}, u32[]{:S(2)}, u32[]{:S(2)}) collective-permute-start(bf16[2048,128]{1,0:T(8,128)(2,1)S(1)} %get-tuple-element.81.refs_3_), channel_id=1, source_target_pairs={{16,0},{17,1},{18,2},{19,3},{20,4},{21,5},{22,6},{23,7},{24,8},{25... | collective-permute-start | bytes 1572872 | tf_op jit(solution)/shard_map/ppermute | solution.py:28
  70.2 46.3 %collective-permute-start.20 = (bf16[2048,128]{1,0:T(8,128)(2,1)S(1)}, bf16[2048,128]{1,0:T(8,128)(2,1)}, u32[]{:S(2)}, u32[]{:S(2)}) collective-permute-start(bf16[2048,128]{1,0:T(8,128)(2,1)S(1)} %get-tuple-element.81.refs_3_), channel_id=1, source_target_pairs={{8,0},{9,1},{10,2},{11,3},{12,4},{13,5},{14,6},{15,7},{16,8},{17,9... | collective-permute-start | bytes 1572872 | tf_op jit(solution)/shard_map/ppermute | solution.py:28
  80.6 48.3 %collective-permute-start.21 = (bf16[2048,128]{1,0:T(8,128)(2,1)S(1)}, bf16[2048,128]{1,0:T(8,128)(2,1)}, u32[]{:S(2)}, u32[]{:S(2)}) collective-permute-start(bf16[2048,128]{1,0:T(8,128)(2,1)S(1)} %get-tuple-element.81.refs_3_), channel_id=1, source_target_pairs={{0,8},{1,9},{2,10},{3,11},{4,12},{5,13},{6,14},{7,15},{8,16},{9,17... | collective-permute-start | bytes 1572872 | tf_op jit(solution)/shard_map/ppermute | solution.py:28
  95.9 34.4 %collective-permute-start.22 = (bf16[2048,128]{1,0:T(8,128)(2,1)S(1)}, bf16[2048,128]{1,0:T(8,128)(2,1)}, u32[]{:S(2)}, u32[]{:S(2)}) collective-permute-start(bf16[2048,128]{1,0:T(8,128)(2,1)S(1)} %get-tuple-element.81.refs_3_), channel_id=1, source_target_pairs={{0,16},{1,17},{2,18},{3,19},{4,20},{5,21},{6,22},{7,23},{8,24},{9,... | collective-permute-start | bytes 1572872 | tf_op jit(solution)/shard_map/ppermute | solution.py:28
  98.0 39.7 %collective-permute-start = (bf16[2048,128]{1,0:T(8,128)(2,1)S(1)}, bf16[2048,128]{1,0:T(8,128)(2,1)}, u32[]{:S(2)}, u32[]{:S(2)}) collective-permute-start(bf16[2048,128]{1,0:T(8,128)(2,1)S(1)} %get-tuple-element.78.refs_3_), channel_id=1, source_target_pairs={{16,0},{17,1},{18,2},{19,3},{20,4},{21,5},{22,6},{23,7},{24,8},{25... | collective-permute-start | bytes 1572872 | tf_op jit(solution)/shard_map/ppermute | solution.py:28
  144.4 90.2 %collective-permute-start.14 = (bf16[4,2048,128]{2,1,0:T(8,128)(2,1)S(1)}, bf16[4,2048,128]{2,1,0:T(8,128)(2,1)}, u32[]{:S(2)}, u32[]{:S(2)}) collective-permute-start(bf16[4,2048,128]{2,1,0:T(8,128)(2,1)S(1)} %bitcast_select_fusion.refs_8_), channel_id=1, source_target_pairs={{0,2},{1,3},{2,0},{3,1},{4,6},{5,7},{6,4},{7,5},{8,10},{9,11},{10,... | collective-permute-start | bytes 6291464 | tf_op jit(solution)/shard_map/ppermute | solution.py:28
  221.4 75.1 %collective-permute-start.13 = (bf16[4,2048,128]{2,1,0:T(8,128)(2,1)S(1)}, bf16[4,2048,128]{2,1,0:T(8,128)(2,1)}, u32[]{:S(2)}, u32[]{:S(2)}) collective-permute-start(bf16[4,2048,128]{2,1,0:T(8,128)(2,1)S(1)} %bitcast_select_fusion.refs_8_), channel_id=1, source_target_pairs={{0,1},{1,0},{2,3},{3,2},{4,5},{5,4},{6,7},{7,6},{8,9},{9,8},{10,11... | collective-permute-start | bytes 6291464 | tf_op jit(solution)/shard_map/ppermute | solution.py:28
  234.6 68.9 %collective-permute-start.15 = (bf16[4,2048,128]{2,1,0:T(8,128)(2,1)}, bf16[4,2048,128]{2,1,0:T(8,128)(2,1)}, u32[]{:S(2)}, u32[]{:S(2)}) collective-permute-start(bf16[4,2048,128]{2,1,0:T(8,128)(2,1)} %collective-permute-done.14.refs_10_), channel_id=1, source_target_pairs={{0,1},{1,0},{2,3},{3,2},{4,5},{5,4},{6,7},{7,6},{8,9},{9,8},{10,11... | collective-permute-start | bytes 6291464 | tf_op jit(solution)/shard_map/ppermute | solution.py:28
  263.4 33.2 %collective-permute-start.43 = (bf16[2048,128]{1,0:T(8,128)(2,1)}, bf16[2048,128]{1,0:T(8,128)(2,1)}, u32[]{:S(2)}, u32[]{:S(2)}) collective-permute-start(bf16[2048,128]{1,0:T(8,128)(2,1)} %collective-permute-done.39.refs_1_), channel_id=1, source_target_pairs={{0,4},{1,5},{2,6},{3,7},{4,0},{5,1},{6,2},{7,3},{8,12},{9,13},{10,... | collective-permute-start | bytes 1572872 | tf_op jit(solution)/shard_map/ppermute | solution.py:28
  326.6 35.5 %collective-permute-start.30 = (bf16[2048,128]{1,0:T(8,128)(2,1)}, bf16[2048,128]{1,0:T(8,128)(2,1)}, u32[]{:S(2)}, u32[]{:S(2)}) collective-permute-start(bf16[2048,128]{1,0:T(8,128)(2,1)} %collective-permute-done.26.refs_3_), channel_id=1, source_target_pairs={{0,4},{1,5},{2,6},{3,7},{4,0},{5,1},{6,2},{7,3},{8,12},{9,13},{10,... | collective-permute-start | bytes 1572872 | tf_op jit(solution)/shard_map/ppermute | solution.py:28
  347.9 33.3 %collective-permute-start.9 = (bf16[2048,128]{1,0:T(8,128)(2,1)S(1)}, bf16[2048,128]{1,0:T(8,128)(2,1)S(1)}, u32[]{:S(2)}, u32[]{:S(2)}) collective-permute-start(bf16[2048,128]{1,0:T(8,128)(2,1)S(1)} %copy-done.32), channel_id=1, source_target_pairs={{0,4},{1,5},{2,6},{3,7},{4,0},{5,1},{6,2},{7,3},{8,12},{9,13},{10,... | collective-permute-start | bytes 1572872 | tf_op jit(solution)/shard_map/ppermute | solution.py:28
  348.9 35.7 %collective-permute-start.10 = (bf16[2048,128]{1,0:T(8,128)(2,1)S(1)}, bf16[2048,128]{1,0:T(8,128)(2,1)}, u32[]{:S(2)}, u32[]{:S(2)}) collective-permute-start(bf16[2048,128]{1,0:T(8,128)(2,1)S(1)} %collective-permute-done.6.refs_1_), channel_id=1, source_target_pairs={{0,4},{1,5},{2,6},{3,7},{4,0},{5,1},{6,2},{7,3},{8,12},{9,13},{10,... | collective-permute-start | bytes 1572872 | tf_op jit(solution)/shard_map/ppermute | solution.py:28
  350.3 45.5 %collective-permute-start.11 = (bf16[2048,128]{1,0:T(8,128)(2,1)}, bf16[2048,128]{1,0:T(8,128)(2,1)}, u32[]{:S(2)}, u32[]{:S(2)}) collective-permute-start(bf16[2048,128]{1,0:T(8,128)(2,1)} %collective-permute-done.7.refs_2_), channel_id=1, source_target_pairs={{0,4},{1,5},{2,6},{3,7},{4,0},{5,1},{6,2},{7,3},{8,12},{9,13},{10,... | collective-permute-start | bytes 1572872 | tf_op jit(solution)/shard_map/ppermute | solution.py:28
  350.9 55.9 %collective-permute-start.12 = (bf16[2048,128]{1,0:T(8,128)(2,1)}, bf16[2048,128]{1,0:T(8,128)(2,1)}, u32[]{:S(2)}, u32[]{:S(2)}) collective-permute-start(bf16[2048,128]{1,0:T(8,128)(2,1)} %collective-permute-done.8.refs_3_), channel_id=1, source_target_pairs={{0,4},{1,5},{2,6},{3,7},{4,0},{5,1},{6,2},{7,3},{8,12},{9,13},{10,... | collective-permute-start | bytes 1572872 | tf_op jit(solution)/shard_map/ppermute | solution.py:28
  362.1 148.8 %collective-permute-start.67 = (bf16[2,512,512]{2,1,0:T(8,128)(2,1)}, bf16[2,512,512]{2,1,0:T(8,128)(2,1)S(1)}, u32[]{:S(2)}, u32[]{:S(2)}) collective-permute-start(bf16[2,512,512]{2,1,0:T(8,128)(2,1)} %get-tuple-element.65), channel_id=1, source_target_pairs={{0,1},{1,0},{2,3},{3,2},{4,5},{5,4},{6,7},{7,6},{8,9},{9,8},{10,11... | collective-permute-start | bytes 3145736 | tf_op jit(solution)/shard_map/ppermute | solution.py:28
  382.0 130.2 %collective-permute-start.46 = (bf16[2,512,512]{2,1,0:T(8,128)(2,1)}, bf16[2,512,512]{2,1,0:T(8,128)(2,1)S(1)}, u32[]{:S(2)}, u32[]{:S(2)}) collective-permute-start(bf16[2,512,512]{2,1,0:T(8,128)(2,1)} %get-tuple-element.55), channel_id=1, source_target_pairs={{0,1},{1,0},{2,3},{3,2},{4,5},{5,4},{6,7},{7,6},{8,9},{9,8},{10,11... | collective-permute-start | bytes 3145736 | tf_op jit(solution)/shard_map/ppermute | solution.py:28
  384.6 129.3 %collective-permute-start.31 = (bf16[2,512,512]{2,1,0:T(8,128)(2,1)}, bf16[2,512,512]{2,1,0:T(8,128)(2,1)S(1)}, u32[]{:S(2)}, u32[]{:S(2)}) collective-permute-start(bf16[2,512,512]{2,1,0:T(8,128)(2,1)} %get-tuple-element.49), channel_id=1, source_target_pairs={{0,1},{1,0},{2,3},{3,2},{4,5},{5,4},{6,7},{7,6},{8,9},{9,8},{10,11... | collective-permute-start | bytes 3145736 | tf_op jit(solution)/shard_map/ppermute | solution.py:28
  429.2 86.3 %collective-permute-start.16 = (bf16[2,512,512]{2,1,0:T(8,128)(2,1)S(1)}, bf16[2,512,512]{2,1,0:T(8,128)(2,1)S(1)}, u32[]{:S(2)}, u32[]{:S(2)}) collective-permute-start(bf16[2,512,512]{2,1,0:T(8,128)(2,1)S(1)} %copy-done.31), channel_id=1, source_target_pairs={{0,1},{1,0},{2,3},{3,2},{4,5},{5,4},{6,7},{7,6},{8,9},{9,8},{10,11... | collective-permute-start | bytes 3145736 | tf_op jit(solution)/shard_map/ppermute | solution.py:28
  (105 other events, 3323.2 us)

commit v3 on v2

--- a/solution.py
+++ b/solution.py
@@ -33,65 +33,59 @@
     def row_swap(self, value, bits):
         return self.move(value, lambda i, j: (i ^ bits, j))
 
-    def group_shift(self, value, step, held=0):
+    def group_swap(self, value, bits, some=None):
         def target(i, j):
             group = i // self.per
-            source, to = group - held, group + step
-            if 0 <= source < self.cols and 0 <= to < self.cols:
-                return (i + step * self.per, j)
+            if some is None or group in some:
+                return ((group ^ bits) * self.per + i % self.per, j)
             return None
 
         return self.move(value, target)
 
 
-def line_start(grid, own):
-    values = {0: own}
-    for far in (2, 1):
-        for sign in (1, -1):
-            if far < grid.cols:
-                values[sign * far] = grid.group_shift(own, sign * far)
-    return values
-
-
-def line_finish(grid, values):
-    for far in range(3, grid.cols):
-        for sign in (1, -1):
-            values[sign * far] = grid.group_shift(
-                values[sign * (far - 1)], sign, held=sign * (far - 1)
-            )
-    return [values[delta] for delta in range(1 - grid.cols, grid.cols)]
-
-
-def pick_kernel(n, where_ref, *refs):
-    values, outs, sems = refs[: 2 * n - 1], refs[2 * n - 1 : 3 * n - 1], refs[3 * n - 1]
+def line_start(grid, own, relayed):
+    if relayed:
+        return [own, grid.group_swap(own, 2), grid.group_swap(own, 1), grid.group_swap(own, 3, (1, 2))]
+    return [own] + [grid.group_swap(own, e) for e in range(grid.cols - 1, 0, -1)]
+
+
+def line_finish(grid, values, relayed):
+    if relayed:
+        own, two, one, near = values
+        return [own, one, two, near, grid.group_swap(two, 1, (1, 2))]
+    return values[:1] + values[:0:-1]
+
+
+def pick_kernel(n, m, where_ref, *refs):
+    values, outs, sems = refs[:m], refs[m : m + n // 2], refs[m + n // 2]
     for d in range(n):
-        for k in range(2 * n - 1):
+        for k in range(m):
 
             @pl.when(where_ref[d] == k)
             def _(d=d, k=k):
-                pltpu.make_async_copy(values[k], outs[d], sems.at[d]).start()
+                pltpu.make_async_copy(values[k], outs[d // 2].at[d % 2], sems.at[d]).start()
 
     for d in range(n):
-        pltpu.make_async_copy(values[0], outs[d], sems.at[d]).wait()
+        pltpu.make_async_copy(values[0], outs[d // 2].at[d % 2], sems.at[d]).wait()
 
 
 def pick(grid, values, where):
-    n = grid.cols
+    n, m = grid.cols, len(values)
     shape = values[0].shape
     if shape[-1] % LANES:
         stacked = jnp.stack(values)
-        return [lax.dynamic_index_in_dim(stacked, where[d], 0, keepdims=False) for d in range(n)]
+        return [jnp.take(stacked, where[d : d + 2], axis=0) for d in range(0, n, 2)]
     size = values[0].size * 2
     return pl.pallas_call(
-        functools.partial(pick_kernel, n),
+        functools.partial(pick_kernel, n, m),
         grid_spec=pltpu.PrefetchScalarGridSpec(
             num_scalar_prefetch=1,
             grid=(1,),
-            in_specs=[pl.BlockSpec(memory_space=pl.ANY)] * (2 * n - 1),
-            out_specs=[pl.BlockSpec(shape, lambda g, w: (0,) * len(shape))] * n,
+            in_specs=[pl.BlockSpec(memory_space=pl.ANY)] * m,
+            out_specs=[pl.BlockSpec((2,) + shape, lambda g, w: (0,) * (len(shape) + 1))] * (n // 2),
             scratch_shapes=[pltpu.SemaphoreType.DMA((n,))],
         ),
-        out_shape=[jax.ShapeDtypeStruct(shape, values[0].dtype)] * n,
+        out_shape=[jax.ShapeDtypeStruct((2,) + shape, values[0].dtype)] * (n // 2),
         cost_estimate=pl.CostEstimate(flops=0, transcendentals=0, bytes_accessed=2 * n * size),
         name="pick",
     )(where, *values)
@@ -102,8 +96,7 @@
     left, refs = refs[:n], refs[n:]
     keep, send, diag_keep, diag_send, right, diag, sems = refs
     col, offset, row = where_ref[0], where_ref[1], where_ref[2]
-    width = pieces[0].shape[1]
-    depth = pieces[0].shape[0]
+    depth, width = pieces[0].shape[1:]
     part = diag.shape[0] // rows_all
     step = pl.program_id(0)
 
@@ -116,7 +109,7 @@
                     pl.ds(pl.multiple_of((offset ^ t) * depth, depth), depth),
                     pl.ds(pl.multiple_of((col ^ d) * width, width), width),
                 ]
-                copies.append(pltpu.make_async_copy(pieces[t * n + d], place, sems.at[t * n + d]))
+                copies.append(pltpu.make_async_copy(pieces[t * n + d].at[d % 2], place, sems.at[t * n + d]))
         for copy in copies:
             copy.start()
         diag[...] = jnp.zeros_like(diag)
@@ -164,7 +157,7 @@
         order_col = col ^ jnp.arange(n)
         order_off = offset ^ jnp.arange(per)
         order_row = row ^ jnp.arange(rows_all)
-        right = jnp.stack([jnp.stack(line) for line in pieces])
+        right = jnp.stack([jnp.stack([value[d % 2] for d, value in enumerate(line)]) for line in pieces])
         right = jnp.take(jnp.take(right, order_off, axis=0), order_col, axis=1)
         right = right.transpose(0, 3, 2, 1, 4).reshape(cols_blk, len(supers) * panel_width)
         product = jnp.dot(inverse_tiles, right, preferred_element_type=jnp.float32)
@@ -229,22 +222,20 @@
     while True:
         moved = grid.col_swap(send, bit)
         yield
-        keep = keep + moved.astype(jnp.float32)
         bit *= 2
         if bit >= grid.cols:
             break
-        send, keep = keep[1::2].astype(jnp.bfloat16), keep[0::2]
-    out.append(keep[0])
-
-
-def reduce_diag(grid, keep, send, out):
-    yield from reduce_panel(grid, keep, send, out)
-    value = out.pop()
+        send = (keep[1::2] + moved[1::2].astype(jnp.float32)).astype(jnp.bfloat16)
+        keep = keep[0::2] + moved[0::2].astype(jnp.float32)
+    out.append(keep[0] + moved[0].astype(jnp.float32))
+
+
+def reduce_rows(grid, value, out):
     bit = 1
     while bit < grid.rows:
-        moved = grid.row_swap(value[1::2], bit)
+        moved = grid.row_swap(value[1::2].astype(jnp.bfloat16), bit)
         yield
-        value = value[0::2] + moved
+        value = value[0::2] + moved.astype(jnp.float32)
         bit *= 2
     out.append(value[0])
 
@@ -271,13 +262,21 @@
     )
     listed = jnp.any(matches, axis=2)
     live = jnp.repeat(listed, TILE, axis=1)
-    masked = jnp.where(
-        live[:, :, None], factor.transpose(1, 0, 2), jnp.zeros((), factor.dtype)
-    )
+
+    def mask(values, live):
+        return jnp.where(live[..., None], values, jnp.zeros((), values.dtype))
 
     together = 1 if width % LANES == 0 else supers
     chunks = [tuple(range(at, at + together)) for at in range(0, supers, together)]
-    where_pick = group - (col ^ jnp.arange(grid.cols, dtype=jnp.int32)) + grid.cols - 1
+    if len(chunks) > 1:
+        first = mask(factor[:, 0], live[0])
+        first, factor = lax.optimization_barrier((first, factor))
+    masked = mask(factor.transpose(1, 0, 2), live)
+    if len(chunks) == 1:
+        first = masked
+    relayed = grid.cols == 4
+    where_pick = group ^ col ^ jnp.arange(grid.cols, dtype=jnp.int32)
+    where_relayed = where_pick + ((where_pick == 3) & ((group == 0) | (group == 3)))
     where_panel = jnp.stack([col, offset, row]).astype(jnp.int32)
 
     def rows_of(chunk):
@@ -288,37 +287,55 @@
     if last:
         jobs += [(last, t) for t in range(1, grid.per)]
     lines, pieces, left = {}, {}, {0: masked}
-    panels, diags = [[] for _ in chunks], [[] for _ in chunks]
+    panels, halves = [[] for _ in chunks], [[] for _ in chunks]
+    ready, closed = set(), set()
     running = []
+    pairs = range(grid.cols // 2)
+
+    def through(k):
+        return relayed and k < len(jobs) - 1
 
     def start(k):
         at, t = jobs[k]
-        lines[k] = line_start(grid, early[t] if t else rows_of(chunks[at]))
+        own = first if k == 0 else early[t] if t else rows_of(chunks[at])
+        lines[k] = line_start(grid, own, through(k))
 
     def spread(k):
-        picked = pick(grid, lines.pop(k), where_pick)
-        pieces[k] = [picked[0]] + [grid.col_swap(picked[d], d) for d in range(1, grid.cols)]
+        picked = pick(grid, lines.pop(k), where_relayed if through(k) else where_pick)
+        pieces[k] = [picked[0]] + [grid.col_swap(picked[p], 2 * p) for p in pairs[1:]]
 
     def across(k, some):
         at, t = jobs[k]
         if last and at == last:
             return
         for t in range(1, grid.per):
-            for d in some:
-                pieces[k, t, d] = grid.row_swap(pieces[k][d], t)
+            for p in some:
+                pieces[k, t, p] = grid.row_swap(pieces[k][p], t)
+
+    def inner(values):
+        return [value for pair in values for value in (pair, grid.col_swap(pair, 1))]
+
+    def close(k):
+        pieces[k] = inner(pieces[k])
+
+    def close_across(k):
+        at, t = jobs[k]
+        if last and at == last:
+            return
+        for t in range(1, grid.per):
+            pieces[k, t] = inner([pieces[k, t, p] for p in pairs])
 
     def multiply(at):
         if last and at == last:
             full = [pieces[k] for k in range(last, len(jobs))]
         else:
-            full = [pieces[at]] + [
-                [pieces[at, t, d] for d in range(grid.cols)] for t in range(1, grid.per)
-            ]
+            full = [pieces[at]] + [pieces[at, t] for t in range(1, grid.per)]
         keep, send, diag_keep, diag_send = panel(
             grid, where_panel, inverse_tiles, full, [left[d] for d in range(grid.cols)], chunks[at]
         )
-        running.append(reduce_diag(grid, diag_keep, diag_send, diags[at]))
+        running.append(reduce_panel(grid, diag_keep, diag_send, halves[at]))
         running.append(reduce_panel(grid, keep, send, panels[at]))
+        advance(running)
 
     start(0)
     bit = grid.cols // 2
@@ -327,45 +344,57 @@
     if last:
         early = {t: grid.row_swap(rows_of(chunks[last]), t) for t in range(1, grid.per)}
     bit //= 2
-    near = [d for d in range(grid.cols) if d < 2]
-    far = [d for d in range(grid.cols) if d >= 2]
-    for k in range(len(jobs)):
-        lines[k] = line_finish(grid, lines[k])
-        if k + 1 < len(jobs):
-            start(k + 1)
-        if k:
-            across(k - 1, far)
+    count = len(jobs)
+    ahead = 1
+    for k in range(count):
+        if k not in ready:
+            lines[k] = line_finish(grid, lines[k], through(k))
+        if ahead == k + 1 < count:
+            start(ahead)
+            ahead += 1
+        if k and k - 1 not in closed:
+            across(k - 1, pairs[1:])
+            close(k - 1)
+        if 2 <= k < count - 2:
+            close_across(k - 2)
+        spread(k)
+        across(k, pairs[:1])
+        while bit:
+            for d in list(left):
+                left[d | bit] = grid.col_swap(left[d], bit)
+            bit //= 2
         advance(running)
-        if k == len(jobs) - 1 and k >= 3:
-            multiply(k - 3)
-        spread(k)
-        across(k, near)
+        if k == count - 3 > 0:
+            start(ahead)
+            ahead += 1
+            multiply(k - 2)
+            lines[k + 1] = line_finish(grid, lines[k + 1], through(k + 1))
+            ready.add(k + 1)
+            across(k, pairs[1:])
+            close(k)
+            closed.add(k)
+        elif k == count - 2 > 1:
+            close_across(k - 2)
+            multiply(k - 2)
+    across(count - 1, pairs[1:])
+    rest = range(max(count - 3, 0), len(chunks))
+    for at in rest:
+        if at == rest[-1]:
+            close(count - 1)
+        close_across(at)
+        multiply(at)
+    while any(not half for half in halves):
         advance(running)
-        if k == 0:
-            while bit:
-                for d in list(left):
-                    left[d | bit] = grid.col_swap(left[d], bit)
-                bit //= 2
-        if 2 <= k < len(jobs) - 2 or (k >= 2 and k == len(jobs) - 2 and False):
-            multiply(k - 2)
-            advance(running)
-    across(len(jobs) - 1, far)
-    done = {at for at in range(len(chunks)) if 2 <= at + 2 < len(jobs) - 2}
-    if len(jobs) >= 4:
-        done.add(len(jobs) - 4)
-    for at in range(len(chunks)):
-        if at not in done:
-            multiply(at)
-            advance(running)
+    diags = []
+    value = jnp.stack([half[0] for half in halves], axis=1)
+    running.insert(0, reduce_rows(grid, value, diags))
     while running:
         advance(running)
     panels = [value[0].reshape(len(chunk), share, -1) for value, chunk in zip(panels, chunks)]
-    diags = [value[0].reshape(len(chunk), -1, width) for value, chunk in zip(diags, chunks)]
-
+    diag_block = inverse_diag + diags[0].reshape(inverse_diag.shape)
     summed = jnp.concatenate(panels, axis=0)
     share_live = lax.dynamic_slice_in_dim(live, col * share, share, 1).astype(jnp.float32)
     inverse_panel = (-summed * share_live[:, :, None]).astype(jnp.bfloat16).transpose(1, 0, 2)
-    diag_block = inverse_diag + jnp.concatenate(diags, axis=0)
     return (inverse_panel, diag_block)
 
 

time: 547 us -> 568 us (1.038)
  waiting for transfers between devices: 252 us -> 335 us
  starting transfers between devices: 178 us -> 112 us
    ppermute x89 -> x69, waiting for transfers between devices: 252 us -> 335 us  [move(): return lax.ppermute(value, AXES, pairs)]
    ppermute x89 -> x69, starting transfers between devices: 178 us -> 112 us  [move(): return lax.ppermute(value, AXES, pairs)]
  transfers between devices with their start and end apart: 89 -> 69, of which waited for: 45 -> 32; matrix products, arithmetic and copies ran while one was open for 1% -> 2% of each run, Pallas kernels for 17% -> 17%
where the time goes in v3:
time: 568 us
  waiting for transfers between devices  335 us (59%)
  starting transfers between devices  112 us (20%)
  Pallas kernels  94.6 us (17%)
  other arithmetic  15.3 us (3%)
  local copies, waits for them, and re-layouts  9.12 us (2%)
    ppermute x69, waiting for transfers between devices, move(): return lax.ppermute(value, AXES, pairs)  335 us
    ppermute x69, starting transfers between devices, move(): return lax.ppermute(value, AXES, pairs)  112 us
    pallas_call x4, Pallas kernels, panel(): pl.pallas_call(functools.partial(panel_kernel, n, per, rows_all), grid_sp...  76.9 us
    pallas_call x5, Pallas kernels, pick(): pl.pallas_call(functools.partial(pick_kernel, n, m), grid_spec=pltpu.Pref...  17.7 us
  transfers between devices with their start and end apart: 69, of which 32 were waited for; matrix products, arithmetic and copies ran while one was open for 2% of the time, Pallas kernels for 17%

profile of v3, /device:TPU:0, one launch (start us, length us, event | category | flops | bytes accessed | tf_op | source)
XLA Modules:
  0.0 567.5 jit_solution(13050953125877182037)
XLA Ops:
  17.6 16.3 %collective-permute-done.42.refs_1_ = bf16[2048,128]{1,0:T(8,128)(2,1)S(1)} collective-permute-done((bf16[2048,128]{1,0:T(8,128)(2,1)S(1)}, bf16[2048,128]{1,0:T(8,128)(2,1)S(1)}, u32[]{:S(2)}, u32[]{:S(2)}) %collective-permute-start.42) | collective-permute-done | bytes 524320 | tf_op jit(solution)/shard_map/ppermute | solution.py:28
  39.2 21.4 %collective-permute-start.16 = (bf16[2048,128]{1,0:T(8,128)(2,1)S(1)}, bf16[2048,128]{1,0:T(8,128)(2,1)}, u32[]{:S(2)}, u32[]{:S(2)}) collective-permute-start(bf16[2048,128]{1,0:T(8,128)(2,1)S(1)} %get-tuple-element.64.refs_0_), channel_id=1, source_target_pairs={{0,8},{1,9},{2,10},{3,11},{4,12},{5,13},{6,14},{7,15},{8,0},{9,1},... | collective-permute-start | bytes 1572872 | tf_op jit(solution)/shard_map/ppermute | solution.py:28
  62.5 18.3 %collective-permute-done.30.refs_2_ = bf16[2048,128]{1,0:T(8,128)(2,1)} collective-permute-done((bf16[2048,128]{1,0:T(8,128)(2,1)S(1)}, bf16[2048,128]{1,0:T(8,128)(2,1)}, u32[]{:S(2)}, u32[]{:S(2)}) %collective-permute-start.30) | collective-permute-done | bytes 524320 | tf_op jit(solution)/shard_map/ppermute | solution.py:28
  80.9 14.6 %collective-permute-start.1 = (bf16[2048,128]{1,0:T(8,128)(2,1)S(1)}, bf16[2048,128]{1,0:T(8,128)(2,1)S(1)}, u32[]{:S(2)}, u32[]{:S(2)}) collective-permute-start(bf16[2048,128]{1,0:T(8,128)(2,1)S(1)} %fusion.3.refs_0_), channel_id=1, source_target_pairs={{0,16},{1,17},{2,18},{3,19},{4,20},{5,21},{6,22},{7,23},{8,24},{9,... | collective-permute-start | bytes 1572872 | tf_op jit(solution)/shard_map/ppermute | solution.py:28
  96.2 20.1 %collective-permute-done.17.refs_2_ = bf16[2048,128]{1,0:T(8,128)(2,1)S(1)} collective-permute-done((bf16[2048,128]{1,0:T(8,128)(2,1)S(1)}, bf16[2048,128]{1,0:T(8,128)(2,1)S(1)}, u32[]{:S(2)}, u32[]{:S(2)}) %collective-permute-start.17) | collective-permute-done | bytes 524320 | tf_op jit(solution)/shard_map/ppermute | solution.py:28
  117.6 10.5 %collective-permute-start.50 = (bf16[2048,128]{1,0:T(8,128)(2,1)}, bf16[2048,128]{1,0:T(8,128)(2,1)}, u32[]{:S(2)}, u32[]{:S(2)}) collective-permute-start(bf16[2048,128]{1,0:T(8,128)(2,1)} %collective-permute-done.49.refs_0_), channel_id=1, source_target_pairs={{0,8},{1,9},{2,10},{3,11},{4,12},{5,13},{6,14},{7,15},{8,0},{9,1},... | collective-permute-start | bytes 1572872 | tf_op jit(solution)/shard_map/ppermute | solution.py:28
  129.2 12.2 %collective-permute-done.1.refs_2_ = bf16[2048,128]{1,0:T(8,128)(2,1)S(1)} collective-permute-done((bf16[2048,128]{1,0:T(8,128)(2,1)S(1)}, bf16[2048,128]{1,0:T(8,128)(2,1)S(1)}, u32[]{:S(2)}, u32[]{:S(2)}) %collective-permute-start.1) | collective-permute-done | bytes 524320 | tf_op jit(solution)/shard_map/ppermute | solution.py:28
  152.3 11.2 %collective-permute-done.50.refs_1_ = bf16[2048,128]{1,0:T(8,128)(2,1)} collective-permute-done((bf16[2048,128]{1,0:T(8,128)(2,1)}, bf16[2048,128]{1,0:T(8,128)(2,1)}, u32[]{:S(2)}, u32[]{:S(2)}) %collective-permute-start.50) | collective-permute-done | bytes 524320 | tf_op jit(solution)/shard_map/ppermute | solution.py:28
  163.4 20.5 %collective-permute-done.51.refs_2_ = bf16[2048,128]{1,0:T(8,128)(2,1)} collective-permute-done((bf16[2048,128]{1,0:T(8,128)(2,1)}, bf16[2048,128]{1,0:T(8,128)(2,1)}, u32[]{:S(2)}, u32[]{:S(2)}) %collective-permute-start.51) | collective-permute-done | bytes 524320 | tf_op jit(solution)/shard_map/ppermute | solution.py:28
  195.4 9.6 %collective-permute-done.19.refs_4_ = bf16[2048,128]{1,0:T(8,128)(2,1)} collective-permute-done((bf16[2048,128]{1,0:T(8,128)(2,1)}, bf16[2048,128]{1,0:T(8,128)(2,1)}, u32[]{:S(2)}, u32[]{:S(2)}) %collective-permute-start.19) | collective-permute-done | bytes 524320 | tf_op jit(solution)/shard_map/ppermute | solution.py:28
  210.4 10.4 %collective-permute-done.3.refs_4_ = bf16[2048,128]{1,0:T(8,128)(2,1)} collective-permute-done((bf16[2048,128]{1,0:T(8,128)(2,1)S(1)}, bf16[2048,128]{1,0:T(8,128)(2,1)}, u32[]{:S(2)}, u32[]{:S(2)}) %collective-permute-start.3) | collective-permute-done | bytes 524320 | tf_op jit(solution)/shard_map/ppermute | solution.py:28
  226.0 29.1 %collective-permute-done.47.refs_2_ = bf16[2,2048,128]{2,1,0:T(8,128)(2,1)} collective-permute-done((bf16[2,2048,128]{2,1,0:T(8,128)(2,1)}, bf16[2,2048,128]{2,1,0:T(8,128)(2,1)}, u32[]{:S(2)}, u32[]{:S(2)}) %collective-permute-start.47) | collective-permute-done | bytes 1048608 | tf_op jit(solution)/shard_map/ppermute | solution.py:28
  260.3 17.3 %collective-permute-done.54.refs_6_ = bf16[2,2048,128]{2,1,0:T(8,128)(2,1)} collective-permute-done((bf16[2,2048,128]{2,1,0:T(8,128)(2,1)}, bf16[2,2048,128]{2,1,0:T(8,128)(2,1)}, u32[]{:S(2)}, u32[]{:S(2)}) %collective-permute-start.54) | collective-permute-done | bytes 1048608 | tf_op jit(solution)/shard_map/ppermute | solution.py:28
  284.7 15.3 %collective-permute-done.34.refs_2_ = bf16[2,2048,128]{2,1,0:T(8,128)(2,1)} collective-permute-done((bf16[2,2048,128]{2,1,0:T(8,128)(2,1)}, bf16[2,2048,128]{2,1,0:T(8,128)(2,1)}, u32[]{:S(2)}, u32[]{:S(2)}) %collective-permute-start.34) | collective-permute-done | bytes 1048608 | tf_op jit(solution)/shard_map/ppermute | solution.py:28
  305.2 17.2 %collective-permute-done.21.refs_2_ = bf16[2,2048,128]{2,1,0:T(8,128)(2,1)S(1)} collective-permute-done((bf16[2,2048,128]{2,1,0:T(8,128)(2,1)}, bf16[2,2048,128]{2,1,0:T(8,128)(2,1)S(1)}, u32[]{:S(2)}, u32[]{:S(2)}) %collective-permute-start.21) | collective-permute-done | bytes 1048608 | tf_op jit(solution)/shard_map/ppermute | solution.py:28
  326.2 18.3 %collective-permute-done.5.refs_2_ = bf16[2,2048,128]{2,1,0:T(8,128)(2,1)} collective-permute-done((bf16[2,2048,128]{2,1,0:T(8,128)(2,1)}, bf16[2,2048,128]{2,1,0:T(8,128)(2,1)}, u32[]{:S(2)}, u32[]{:S(2)}) %collective-permute-start.5) | collective-permute-done | bytes 1048608 | tf_op jit(solution)/shard_map/ppermute | solution.py:28
  349.9 23.2 %collective-permute-done.38.refs_6_ = bf16[2,2048,128]{2,1,0:T(8,128)(2,1)} collective-permute-done((bf16[2,2048,128]{2,1,0:T(8,128)(2,1)}, bf16[2,2048,128]{2,1,0:T(8,128)(2,1)}, u32[]{:S(2)}, u32[]{:S(2)}) %collective-permute-start.38) | collective-permute-done | bytes 1048608 | tf_op jit(solution)/shard_map/ppermute | solution.py:28
  374.6 21.0 %collective-permute-done.25.refs_6_ = bf16[2,2048,128]{2,1,0:T(8,128)(2,1)} collective-permute-done((bf16[2,2048,128]{2,1,0:T(8,128)(2,1)}, bf16[2,2048,128]{2,1,0:T(8,128)(2,1)}, u32[]{:S(2)}, u32[]{:S(2)}) %collective-permute-start.25) | collective-permute-done | bytes 1048608 | tf_op jit(solution)/shard_map/ppermute | solution.py:28
  397.5 19.3 %panel.7 = (f32[2,512,512]{2,1,0:T(8,128)}, bf16[2,512,512]{2,1,0:T(8,128)(2,1)}, f32[2,8,64,128]{3,2,1,0:T(8,128)}, bf16[2,8,64,128]{3,2,1,0:T(8,128)(2,1)}) custom-call(s32[3]{0:T(128)} %pad_add_fusion.where_ref, bf16[2048,4096]{1,0:T(8,128)(2,1)} %a_ref.7, bf16[2,2048,128]{2,1,0:T(8,128)(2,1)} %get-tuple-element.44.refs_0_, ...), custom_call_target="tpu_custom_call" | custom-call | flops 9663676416 | bytes 26214400 | tf_op jit(solution)/shard_map/panel/pallas_call | solution.py:185
  418.1 19.2 %panel.6 = (f32[2,512,512]{2,1,0:T(8,128)}, bf16[2,512,512]{2,1,0:T(8,128)(2,1)}, f32[2,8,64,128]{3,2,1,0:T(8,128)}, bf16[2,8,64,128]{3,2,1,0:T(8,128)(2,1)}) custom-call(s32[3]{0:T(128)} %pad_add_fusion.where_ref, bf16[2048,4096]{1,0:T(8,128)(2,1)} %a_ref.7, bf16[2,2048,128]{2,1,0:T(8,128)(2,1)} %get-tuple-element.40.refs_0_, ...), custom_call_target="tpu_custom_call" | custom-call | flops 9663676416 | bytes 26214400 | tf_op jit(solution)/shard_map/panel/pallas_call | solution.py:185
  437.8 19.2 %panel.5 = (f32[2,512,512]{2,1,0:T(8,128)}, bf16[2,512,512]{2,1,0:T(8,128)(2,1)}, f32[2,8,64,128]{3,2,1,0:T(8,128)}, bf16[2,8,64,128]{3,2,1,0:T(8,128)(2,1)}) custom-call(s32[3]{0:T(128)} %pad_add_fusion.where_ref, bf16[2048,4096]{1,0:T(8,128)(2,1)} %a_ref.7, bf16[2,2048,128]{2,1,0:T(8,128)(2,1)} %get-tuple-element.36.refs_0_, ...), custom_call_target="tpu_custom_call" | custom-call | flops 9663676416 | bytes 26214400 | tf_op jit(solution)/shard_map/panel/pallas_call | solution.py:185
  458.6 19.2 %panel.4 = (f32[2,512,512]{2,1,0:T(8,128)}, bf16[2,512,512]{2,1,0:T(8,128)(2,1)}, f32[2,8,64,128]{3,2,1,0:T(8,128)}, bf16[2,8,64,128]{3,2,1,0:T(8,128)(2,1)}) custom-call(s32[3]{0:T(128)} %pad_add_fusion.where_ref, bf16[2048,4096]{1,0:T(8,128)(2,1)} %a_ref.7, bf16[2,2048,128]{2,1,0:T(8,128)(2,1)} %get-tuple-element.31.refs_0_, ...), custom_call_target="tpu_custom_call" | custom-call | flops 9663676416 | bytes 26214400 | tf_op jit(solution)/shard_map/panel/pallas_call | solution.py:185
  533.9 10.0 %collective-permute-done.41 = bf16[1,512,512]{2,1,0:T(8,128)(2,1)S(1)} collective-permute-done((bf16[1,512,512]{2,1,0:T(8,128)(2,1)S(1)}, bf16[1,512,512]{2,1,0:T(8,128)(2,1)S(1)}, u32[]{:S(2)}, u32[]{:S(2)}) %collective-permute-start.41) | collective-permute-done | bytes 524320 | tf_op jit(solution)/shard_map/ppermute | solution.py:28
  545.1 10.0 %collective-permute-done.28 = bf16[1,512,512]{2,1,0:T(8,128)(2,1)S(1)} collective-permute-done((bf16[1,512,512]{2,1,0:T(8,128)(2,1)S(1)}, bf16[1,512,512]{2,1,0:T(8,128)(2,1)S(1)}, u32[]{:S(2)}, u32[]{:S(2)}) %collective-permute-start.28) | collective-permute-done | bytes 524320 | tf_op jit(solution)/shard_map/ppermute | solution.py:28
  (224 shorter events, 162.9 us)
Async XLA Ops:
  14.0 46.7 %collective-permute-start.49 = (bf16[2048,128]{1,0:T(8,128)(2,1)S(1)}, bf16[2048,128]{1,0:T(8,128)(2,1)}, u32[]{:S(2)}, u32[]{:S(2)}) collective-permute-start(bf16[2048,128]{1,0:T(8,128)(2,1)S(1)} %get-tuple-element.65.refs_0_), channel_id=1, source_target_pairs={{0,4},{1,5},{2,6},{3,7},{4,0},{5,1},{6,2},{7,3},{8,12},{9,13},{10,... | collective-permute-start | bytes 1572872 | tf_op jit(solution)/shard_map/ppermute | solution.py:28
  15.5 46.2 %collective-permute-start.29 = (bf16[2048,128]{1,0:T(8,128)(2,1)S(1)}, bf16[2048,128]{1,0:T(8,128)(2,1)S(1)}, u32[]{:S(2)}, u32[]{:S(2)}) collective-permute-start(bf16[2048,128]{1,0:T(8,128)(2,1)S(1)} %get-tuple-element.66.refs_0_), channel_id=1, source_target_pairs={{0,8},{1,9},{2,10},{3,11},{4,12},{5,13},{6,14},{7,15},{8,0},{9,1},... | collective-permute-start | bytes 1572872 | tf_op jit(solution)/shard_map/ppermute | solution.py:28
  34.0 46.9 %collective-permute-start.30 = (bf16[2048,128]{1,0:T(8,128)(2,1)S(1)}, bf16[2048,128]{1,0:T(8,128)(2,1)}, u32[]{:S(2)}, u32[]{:S(2)}) collective-permute-start(bf16[2048,128]{1,0:T(8,128)(2,1)S(1)} %get-tuple-element.66.refs_0_), channel_id=1, source_target_pairs={{0,16},{1,17},{2,18},{3,19},{4,20},{5,21},{6,22},{7,23},{8,24},{9,... | collective-permute-start | bytes 1572872 | tf_op jit(solution)/shard_map/ppermute | solution.py:28
  39.2 56.3 %collective-permute-start.16 = (bf16[2048,128]{1,0:T(8,128)(2,1)S(1)}, bf16[2048,128]{1,0:T(8,128)(2,1)}, u32[]{:S(2)}, u32[]{:S(2)}) collective-permute-start(bf16[2048,128]{1,0:T(8,128)(2,1)S(1)} %get-tuple-element.64.refs_0_), channel_id=1, source_target_pairs={{0,8},{1,9},{2,10},{3,11},{4,12},{5,13},{6,14},{7,15},{8,0},{9,1},... | collective-permute-start | bytes 1572872 | tf_op jit(solution)/shard_map/ppermute | solution.py:28
  60.7 55.6 %collective-permute-start.17 = (bf16[2048,128]{1,0:T(8,128)(2,1)S(1)}, bf16[2048,128]{1,0:T(8,128)(2,1)S(1)}, u32[]{:S(2)}, u32[]{:S(2)}) collective-permute-start(bf16[2048,128]{1,0:T(8,128)(2,1)S(1)} %get-tuple-element.64.refs_0_), channel_id=1, source_target_pairs={{0,16},{1,17},{2,18},{3,19},{4,20},{5,21},{6,22},{7,23},{8,24},{9,... | collective-permute-start | bytes 1572872 | tf_op jit(solution)/shard_map/ppermute | solution.py:28
  61.7 55.9 %collective-permute-start.18 = (bf16[2048,128]{1,0:T(8,128)(2,1)S(1)}, bf16[2048,128]{1,0:T(8,128)(2,1)S(1)}, u32[]{:S(2)}, u32[]{:S(2)}) collective-permute-start(bf16[2048,128]{1,0:T(8,128)(2,1)S(1)} %get-tuple-element.64.refs_0_), channel_id=1, source_target_pairs={{8,16},{9,17},{10,18},{11,19},{12,20},{13,21},{14,22},{15,23},{16,... | collective-permute-start | bytes 1572872 | tf_op jit(solution)/shard_map/ppermute | solution.py:28
  80.8 47.3 %collective-permute-start = (bf16[2048,128]{1,0:T(8,128)(2,1)S(1)}, bf16[2048,128]{1,0:T(8,128)(2,1)S(1)}, u32[]{:S(2)}, u32[]{:S(2)}) collective-permute-start(bf16[2048,128]{1,0:T(8,128)(2,1)S(1)} %fusion.3.refs_0_), channel_id=1, source_target_pairs={{0,8},{1,9},{2,10},{3,11},{4,12},{5,13},{6,14},{7,15},{8,0},{9,1},... | collective-permute-start | bytes 1572872 | tf_op jit(solution)/shard_map/ppermute | solution.py:28
  80.9 60.5 %collective-permute-start.1 = (bf16[2048,128]{1,0:T(8,128)(2,1)S(1)}, bf16[2048,128]{1,0:T(8,128)(2,1)S(1)}, u32[]{:S(2)}, u32[]{:S(2)}) collective-permute-start(bf16[2048,128]{1,0:T(8,128)(2,1)S(1)} %fusion.3.refs_0_), channel_id=1, source_target_pairs={{0,16},{1,17},{2,18},{3,19},{4,20},{5,21},{6,22},{7,23},{8,24},{9,... | collective-permute-start | bytes 1572872 | tf_op jit(solution)/shard_map/ppermute | solution.py:28
  95.5 49.3 %collective-permute-start.2 = (bf16[2048,128]{1,0:T(8,128)(2,1)S(1)}, bf16[2048,128]{1,0:T(8,128)(2,1)S(1)}, u32[]{:S(2)}, u32[]{:S(2)}) collective-permute-start(bf16[2048,128]{1,0:T(8,128)(2,1)S(1)} %fusion.3.refs_0_), channel_id=1, source_target_pairs={{8,16},{9,17},{10,18},{11,19},{12,20},{13,21},{14,22},{15,23},{16,... | collective-permute-start | bytes 1572872 | tf_op jit(solution)/shard_map/ppermute | solution.py:28
  117.6 45.8 %collective-permute-start.50 = (bf16[2048,128]{1,0:T(8,128)(2,1)}, bf16[2048,128]{1,0:T(8,128)(2,1)}, u32[]{:S(2)}, u32[]{:S(2)}) collective-permute-start(bf16[2048,128]{1,0:T(8,128)(2,1)} %collective-permute-done.49.refs_0_), channel_id=1, source_target_pairs={{0,8},{1,9},{2,10},{3,11},{4,12},{5,13},{6,14},{7,15},{8,0},{9,1},... | collective-permute-start | bytes 1572872 | tf_op jit(solution)/shard_map/ppermute | solution.py:28
  128.1 55.8 %collective-permute-start.51 = (bf16[2048,128]{1,0:T(8,128)(2,1)}, bf16[2048,128]{1,0:T(8,128)(2,1)}, u32[]{:S(2)}, u32[]{:S(2)}) collective-permute-start(bf16[2048,128]{1,0:T(8,128)(2,1)} %collective-permute-done.49.refs_0_), channel_id=1, source_target_pairs={{0,16},{1,17},{2,18},{3,19},{4,20},{5,21},{6,22},{7,23},{8,24},{9,... | collective-permute-start | bytes 1572872 | tf_op jit(solution)/shard_map/ppermute | solution.py:28
  145.7 48.2 %collective-permute-start.32 = (bf16[2048,128]{1,0:T(8,128)(2,1)}, bf16[2048,128]{1,0:T(8,128)(2,1)}, u32[]{:S(2)}, u32[]{:S(2)}) collective-permute-start(bf16[2048,128]{1,0:T(8,128)(2,1)} %collective-permute-done.30.refs_2_), channel_id=1, source_target_pairs={{8,0},{9,1},{10,2},{11,3},{12,4},{13,5},{14,6},{15,7},{16,24},{17,... | collective-permute-start | bytes 1572872 | tf_op jit(solution)/shard_map/ppermute | solution.py:28
  147.5 57.5 %collective-permute-start.19 = (bf16[2048,128]{1,0:T(8,128)(2,1)}, bf16[2048,128]{1,0:T(8,128)(2,1)}, u32[]{:S(2)}, u32[]{:S(2)}) collective-permute-start(bf16[2048,128]{1,0:T(8,128)(2,1)} %copy-done.19), channel_id=1, source_target_pairs={{8,0},{9,1},{10,2},{11,3},{12,4},{13,5},{14,6},{15,7},{16,24},{17,... | collective-permute-start | bytes 1572872 | tf_op jit(solution)/shard_map/ppermute | solution.py:28
  163.4 57.4 %collective-permute-start.46 = (bf16[2,2048,128]{2,1,0:T(8,128)(2,1)}, bf16[2,2048,128]{2,1,0:T(8,128)(2,1)}, u32[]{:S(2)}, u32[]{:S(2)}) collective-permute-start(bf16[2,2048,128]{2,1,0:T(8,128)(2,1)} %get-tuple-element.44.refs_0_), channel_id=1, source_target_pairs={{0,1},{1,0},{2,3},{3,2},{4,5},{5,4},{6,7},{7,6},{8,9},{9,8},{10,11... | collective-permute-start | bytes 3145736 | tf_op jit(solution)/shard_map/ppermute | solution.py:28
  183.9 95.1 %collective-permute-start.11 = (bf16[4,2048,128]{2,1,0:T(8,128)(2,1)S(1)}, bf16[4,2048,128]{2,1,0:T(8,128)(2,1)}, u32[]{:S(2)}, u32[]{:S(2)}) collective-permute-start(bf16[4,2048,128]{2,1,0:T(8,128)(2,1)S(1)} %bitcast_select_fusion.refs_8_), channel_id=1, source_target_pairs={{0,1},{1,0},{2,3},{3,2},{4,5},{5,4},{6,7},{7,6},{8,9},{9,8},{10,11... | collective-permute-start | bytes 6291464 | tf_op jit(solution)/shard_map/ppermute | solution.py:28
  183.9 95.1 %collective-permute-start.12 = (bf16[4,2048,128]{2,1,0:T(8,128)(2,1)S(1)}, bf16[4,2048,128]{2,1,0:T(8,128)(2,1)}, u32[]{:S(2)}, u32[]{:S(2)}) collective-permute-start(bf16[4,2048,128]{2,1,0:T(8,128)(2,1)S(1)} %bitcast_select_fusion.refs_8_), channel_id=1, source_target_pairs={{0,2},{1,3},{2,0},{3,1},{4,6},{5,7},{6,4},{7,5},{8,10},{9,11},{10,... | collective-permute-start | bytes 6291464 | tf_op jit(solution)/shard_map/ppermute | solution.py:28
  193.8 61.2 %collective-permute-start.47 = (bf16[2,2048,128]{2,1,0:T(8,128)(2,1)}, bf16[2,2048,128]{2,1,0:T(8,128)(2,1)}, u32[]{:S(2)}, u32[]{:S(2)}) collective-permute-start(bf16[2,2048,128]{2,1,0:T(8,128)(2,1)} %get-tuple-element.45), channel_id=1, source_target_pairs={{0,2},{1,3},{2,0},{3,1},{4,6},{5,7},{6,4},{7,5},{8,10},{9,11},{10,... | collective-permute-start | bytes 3145736 | tf_op jit(solution)/shard_map/ppermute | solution.py:28
  220.8 56.7 %collective-permute-start.54 = (bf16[2,2048,128]{2,1,0:T(8,128)(2,1)}, bf16[2,2048,128]{2,1,0:T(8,128)(2,1)}, u32[]{:S(2)}, u32[]{:S(2)}) collective-permute-start(bf16[2,2048,128]{2,1,0:T(8,128)(2,1)} %get-tuple-element.47), channel_id=1, source_target_pairs={{0,2},{1,3},{2,0},{3,1},{4,6},{5,7},{6,4},{7,5},{8,10},{9,11},{10,... | collective-permute-start | bytes 3145736 | tf_op jit(solution)/shard_map/ppermute | solution.py:28
  280.6 45.5 %collective-permute-start.23 = (bf16[2,2048,128]{2,1,0:T(8,128)(2,1)}, bf16[2,2048,128]{2,1,0:T(8,128)(2,1)}, u32[]{:S(2)}, u32[]{:S(2)}) collective-permute-start(bf16[2,2048,128]{2,1,0:T(8,128)(2,1)} %get-tuple-element.36.refs_0_), channel_id=1, source_target_pairs={{0,4},{1,5},{2,6},{3,7},{4,0},{5,1},{6,2},{7,3},{8,12},{9,13},{10,... | collective-permute-start | bytes 3145736 | tf_op jit(solution)/shard_map/ppermute | solution.py:28
  326.2 70.0 %collective-permute-start.13 = (bf16[4,2048,128]{2,1,0:T(8,128)(2,1)}, bf16[4,2048,128]{2,1,0:T(8,128)(2,1)S(1)}, u32[]{:S(2)}, u32[]{:S(2)}) collective-permute-start(bf16[4,2048,128]{2,1,0:T(8,128)(2,1)} %collective-permute-done.12.refs_10_), channel_id=1, source_target_pairs={{0,1},{1,0},{2,3},{3,2},{4,5},{5,4},{6,7},{7,6},{8,9},{9,8},{10,11... | collective-permute-start | bytes 6291464 | tf_op jit(solution)/shard_map/ppermute | solution.py:28
  348.2 47.3 %collective-permute-start.25 = (bf16[2,2048,128]{2,1,0:T(8,128)(2,1)}, bf16[2,2048,128]{2,1,0:T(8,128)(2,1)}, u32[]{:S(2)}, u32[]{:S(2)}) collective-permute-start(bf16[2,2048,128]{2,1,0:T(8,128)(2,1)} %copy-done.27), channel_id=1, source_target_pairs={{0,4},{1,5},{2,6},{3,7},{4,0},{5,1},{6,2},{7,3},{8,12},{9,13},{10,... | collective-permute-start | bytes 3145736 | tf_op jit(solution)/shard_map/ppermute | solution.py:28
  348.8 68.1 %collective-permute-start.22 = (bf16[2,2048,128]{2,1,0:T(8,128)(2,1)}, bf16[2,2048,128]{2,1,0:T(8,128)(2,1)}, u32[]{:S(2)}, u32[]{:S(2)}) collective-permute-start(bf16[2,2048,128]{2,1,0:T(8,128)(2,1)} %copy-done.27), channel_id=1, source_target_pairs={{0,1},{1,0},{2,3},{3,2},{4,5},{5,4},{6,7},{7,6},{8,9},{9,8},{10,11... | collective-permute-start | bytes 3145736 | tf_op jit(solution)/shard_map/ppermute | solution.py:28
  349.7 67.7 %collective-permute-start.24 = (bf16[2,2048,128]{2,1,0:T(8,128)(2,1)}, bf16[2,2048,128]{2,1,0:T(8,128)(2,1)}, u32[]{:S(2)}, u32[]{:S(2)}) collective-permute-start(bf16[2,2048,128]{2,1,0:T(8,128)(2,1)} %collective-permute-done.23.refs_4_), channel_id=1, source_target_pairs={{0,1},{1,0},{2,3},{3,2},{4,5},{5,4},{6,7},{7,6},{8,9},{9,8},{10,11... | collective-permute-start | bytes 3145736 | tf_op jit(solution)/shard_map/ppermute | solution.py:28
  373.1 44.5 %collective-permute-start.9 = (bf16[2,2048,128]{2,1,0:T(8,128)(2,1)}, bf16[2,2048,128]{2,1,0:T(8,128)(2,1)}, u32[]{:S(2)}, u32[]{:S(2)}) collective-permute-start(bf16[2,2048,128]{2,1,0:T(8,128)(2,1)} %collective-permute-done.5.refs_2_), channel_id=1, source_target_pairs={{0,4},{1,5},{2,6},{3,7},{4,0},{5,1},{6,2},{7,3},{8,12},{9,13},{10,... | collective-permute-start | bytes 3145736 | tf_op jit(solution)/shard_map/ppermute | solution.py:28
  (75 other events, 2381.1 us)
